TPU v7x, 256 devices: a whole 4x4x8 slice. The times are simulated.
256 devices in a mesh: src: 16 (over z, core), tgt: 16 (over y, x).
Axes of the slice: x: 4, y: 4, z: 8, core: 2. Of those that a mesh axis runs over, the one named last changes fastest.
Arguments:
- source: float32 [32, 16384], P(None, ('src', 'tgt')), may hold values from -2 to 2
- target: float32 [32, 26624], P(None, ('tgt', 'src')), may hold values from -2 to 2
- target_pot: float32 [26624], P(('tgt', 'src')), may hold values from -1 to 8
- source_logw: float32 [16384], P(('src', 'tgt')), may hold values from -14 to -9
- target_logw: float32 [26624], P(('tgt', 'src')), may hold values from -14 to -9
Outputs:
- f_new: float32 [16384], P(('src', 'tgt'))
- g_new: float32 [26624], P(('tgt', 'src'))
- projection: float32 [32, 16384], P(None, ('src', 'tgt'))
All inputs are finite; a program needn't handle non-finite values.
Results may differ from a plain program's by a relative error of at most 0.0003.
Values sent between devices are 32-bit elements; how exact they have to be, the bound alone decides.
A program may use at most 64 MiB of HBM per device.

v0:
```python
import math

import jax
import jax.numpy as jnp
from jax import lax
from jax.sharding import PartitionSpec as P

EPSILON = 0.05
HIGHEST = lax.Precision.HIGHEST


def cost_scores(row_cells, col_cells, col_sq, col_pot, col_logw):
    cross_term = lax.dot_general(
        row_cells,
        col_cells,
        (((0,), (0,)), ((), ())),
        precision=HIGHEST,
        preferred_element_type=jnp.float32,
    )
    cost_tile = jnp.sum(row_cells * row_cells, 0)[:, None] + col_sq[None, :] - 2.0 * cross_term
    return (col_pot[None, :] - cost_tile) / EPSILON + col_logw[None, :]


def log_sums(row_cells, col_cells, col_pot, col_logw, weighted):
    feat_dim, row_count = row_cells.shape
    row_block = math.gcd(row_count, 512)
    col_sq = jnp.sum(col_cells * col_cells, 0)
    blocks = row_cells.reshape(feat_dim, row_count // row_block, row_block).transpose(1, 0, 2)

    def one_block(cells_block):
        scores = cost_scores(cells_block, col_cells, col_sq, col_pot, col_logw)
        row_top = jnp.max(scores, 1)
        kernel = jnp.exp(scores - row_top[:, None])
        totals = jnp.sum(kernel, 1)
        if weighted:
            moments = lax.dot_general(
                col_cells,
                kernel,
                (((1,), (1,)), ((), ())),
                precision=HIGHEST,
                preferred_element_type=jnp.float32,
            )
            return (row_top, totals, moments)
        return (row_top, totals)

    result = lax.map(one_block, blocks)
    row_top = result[0].reshape(row_count)
    totals = result[1].reshape(row_count)
    if weighted:
        moments = result[2].transpose(1, 0, 2).reshape(feat_dim, row_count)
        return (row_top, totals, moments)
    return (row_top, totals)


def body(source, target, target_pot, source_logw, target_logw):
    src_cells, src_logw = (
        lax.all_gather(source, "tgt", axis=1, tiled=True),
        lax.all_gather(source_logw, "tgt", axis=0, tiled=True),
    )
    tgt_cells, tgt_pot, tgt_logw = (
        lax.all_gather(target, "src", axis=1, tiled=True),
        lax.all_gather(target_pot, "src", axis=0, tiled=True),
        lax.all_gather(target_logw, "src", axis=0, tiled=True),
    )
    row_top, row_totals = log_sums(src_cells, tgt_cells, tgt_pot, tgt_logw, False)
    highest = lax.pmax(row_top, "tgt")
    row_totals = lax.psum(row_totals * jnp.exp(row_top - highest), "tgt")
    row_top = highest
    f_block = -EPSILON * (row_top + jnp.log(row_totals))
    col_top, col_totals = log_sums(tgt_cells, src_cells, f_block, src_logw, False)
    col_highest = lax.pmax(col_top, "src")
    col_totals = lax.psum(col_totals * jnp.exp(col_top - col_highest), "src")
    col_top = col_highest
    g_block = -EPSILON * (col_top + jnp.log(col_totals))
    mine_rows = source.shape[1]
    mine_cols = target.shape[1]
    f_new = lax.dynamic_slice_in_dim(f_block, lax.axis_index("tgt") * mine_rows, mine_rows)
    g_new = lax.dynamic_slice_in_dim(g_block, lax.axis_index("src") * mine_cols, mine_cols)
    proj_top, proj_totals, moments = log_sums(src_cells, tgt_cells, g_block, tgt_logw, True)
    proj_highest = lax.pmax(proj_top, "tgt")
    rescale = jnp.exp(proj_top - proj_highest)
    moments_mine, totals_mine = (
        lax.psum_scatter(moments * rescale[None, :], "tgt", scatter_dimension=1, tiled=True),
        lax.psum_scatter(proj_totals * rescale, "tgt", scatter_dimension=0, tiled=True),
    )
    projection = moments_mine / totals_mine[None, :]
    return (f_new, g_new, projection)


def solution(mesh):
    return jax.shard_map(
        body,
        mesh=mesh,
        in_specs=(
            P(None, ("src", "tgt")),
            P(None, ("tgt", "src")),
            P(("tgt", "src")),
            P(("src", "tgt")),
            P(("tgt", "src")),
        ),
        out_specs=(P(("src", "tgt")), P(("tgt", "src")), P(None, ("src", "tgt"))),
        check_vma=False,
    )
```

profile of v0, /device:TPU:1, one launch (start us, length us, event | category | flops | bytes accessed | tf_op | source)
XLA Modules:
  0.0 446.0 jit_solution(15336664736178391552)
XLA Ops:
  7.3 19.7 %all-gather = f32[16,64,32]{1,2,0:T(8,128)S(1)} all-gather(f32[1,64,32]{1,2,0:T(8,128)} %bitcast.127), channel_id=1, replica_groups=mesh['src'=16,'tgt'=16] {'tgt'}, dimensions={0}, use_global_device_ids=true | all-gather | bytes 139264 | tf_op jit(solution)/shard_map/all_gather | solution.py:57
  28.1 26.6 %all-gather.1 = f32[16,104,32]{1,2,0:T(8,128)S(1)} all-gather(f32[1,104,32]{1,2,0:T(8,128)} %bitcast.128), channel_id=1, replica_groups=mesh['src'=16,'tgt'=16] {'src'}, dimensions={0}, use_global_device_ids=true | all-gather | bytes 226304 | tf_op jit(solution)/shard_map/all_gather | solution.py:61
  55.7 1.6 multiply_reduce_fusion.1
  57.2 1.7 reshape.54
  60.8 42.5 %all-reduce.5 = (f32[1664]{0:T(1024)}, f32[1664]{0:T(1024)}) all-reduce(f32[1664]{0:T(1024)S(1)} %dynamic-update-slice, f32[1664]{0:T(1024)S(1)} %dynamic-update-slice.1), channel_id=1, replica_groups=mesh['src'=16,'tgt'=16] {'src'}, use_global_device_ids=true, to_apply=%add | all-reduce | flops 3328 | bytes 26624
  104.5 15.7 %while.38 = (s32[]{:T(128)}, f32[2,512]{1,0:T(2,128)}, f32[2,512]{1,0:T(2,128)}, f32[1664]{0:T(1024)}, f32[2,32,512]{2,1,0:T(8,128)S(1)}, /*index=5*/f32[1664]{0...) while((s32[]{:T(128)}, f32[2,512]{1,0:T(2,128)}, f32[2,512]{1,0:T(2,128)}, ...), condition=%wide.region_5.6_spmd, body=%wide.region_1.5_spmd.sunk | while | flops 334854656 | bytes 7198333 | solution.py:46
  104.5 4.6 %fusion.41 = (f32[512]{0:T(512)S(1)}, f32[512,1664]{1,0:T(8,128)S(1)}) fusion(f32[1664]{0:T(1024)} %get-tuple-element.476, f32[32,1664]{1,0:T(8,128)} %get-tuple-element.475, f32[2,32,512]{2,1,0:T(8,128)S(1)} %get-tuple-element.473, s32[]{:T(128)S(6)} %copy.48, f32[1664]{0:T(1024)} %get-tuple-element.474, f32[512]{0:T(512)S(1)} %fusion.40, ...), kind=kOutput, calls=%fused_computation.37.clone.1 | convolution fusion | flops 333118976 | bytes 3710468 | tf_op jit(solution)/shard_map/while/body/eval_jaxpr/dot_general | solution.py:13
  109.2 1.3 dynamic_update_slice.32
  111.1 1.3 dynamic_update_slice.33
  112.4 4.6 %fusion.41 = (f32[512]{0:T(512)S(1)}, f32[512,1664]{1,0:T(8,128)S(1)}) fusion(f32[1664]{0:T(1024)} %get-tuple-element.476, f32[32,1664]{1,0:T(8,128)} %get-tuple-element.475, f32[2,32,512]{2,1,0:T(8,128)S(1)} %get-tuple-element.473, s32[]{:T(128)S(6)} %copy.48, f32[1664]{0:T(1024)} %get-tuple-element.474, f32[512]{0:T(512)S(1)} %fusion.40, ...), kind=kOutput, calls=%fused_computation.37.clone.1 | convolution fusion | flops 333118976 | bytes 3710468 | tf_op jit(solution)/shard_map/while/body/eval_jaxpr/dot_general | solution.py:13
  117.0 1.3 dynamic_update_slice.32
  118.9 1.3 dynamic_update_slice.33
  120.9 31.0 %pmax.21 = f32[1024]{0:T(1024)S(1)} all-reduce(f32[1024]{0:T(1024)S(1)} %bitcast.123), channel_id=1, replica_groups=mesh['src'=16,'tgt'=16] {'tgt'}, use_global_device_ids=true, to_apply=%region_6.7 | all-reduce | flops 1024 | bytes 8192 | tf_op jit(solution)/shard_map/pmax | solution.py:66
  152.6 1.3 fusion.21
  155.4 29.0 %all-reduce.4 = (f32[1024]{0:T(1024)S(1)}, f32[1024]{0:T(1024)S(1)}) all-reduce(f32[1024]{0:T(1024)S(1)} %exponential_multiply_fusion, f32[1024]{0:T(1024)S(1)} %dynamic-update-slice.2), channel_id=1, replica_groups=mesh['src'=16,'tgt'=16] {'tgt'}, use_global_device_ids=true, to_apply=%region_7.8 | all-reduce | flops 2048 | bytes 16384 | tf_op jit(solution)/shard_map/psum | solution.py:67
  184.5 54.8 %while.39 = (s32[]{:T(128)}, f32[13,128]{1,0:T(8,128)S(1)}, f32[13,128]{1,0:T(8,128)}, f32[1024]{0:T(1024)S(1)}, f32[13,32,128]{2,0,1:T(8,128)}, /*index=5*/f32[...) while((s32[]{:T(128)}, f32[13,128]{1,0:T(8,128)S(1)}, f32[13,128]{1,0:T(8,128)}, ...), condition=%wide.region_13.14_spmd, body=%wide.region_9.13_spmd.sunk | while | flops 51519104 | bytes 1262201 | solution.py:46
  184.5 0.9 constant_dynamic-slice_fusion.2
  185.4 1.7 fusion.44
  187.4 1.3 dynamic_update_slice.35
  188.7 0.9 constant_dynamic-slice_fusion.2
  189.6 1.7 fusion.44
  191.6 1.3 dynamic_update_slice.35
  192.9 0.9 constant_dynamic-slice_fusion.2
  193.9 1.7 fusion.44
  195.8 1.3 dynamic_update_slice.35
  198.1 1.7 fusion.44
  200.0 1.3 dynamic_update_slice.35
  202.3 1.7 fusion.44
  204.2 1.3 dynamic_update_slice.35
  205.5 0.9 constant_dynamic-slice_fusion.2
  206.5 1.7 fusion.44
  208.5 1.3 dynamic_update_slice.35
  209.8 0.9 constant_dynamic-slice_fusion.2
  210.7 1.7 fusion.44
  212.7 1.3 dynamic_update_slice.35
  214.0 0.9 constant_dynamic-slice_fusion.2
  214.9 1.7 fusion.44
  216.9 1.3 dynamic_update_slice.35
  219.1 1.7 fusion.44
  221.1 1.3 dynamic_update_slice.35
  223.3 1.7 fusion.44
  225.3 1.3 dynamic_update_slice.35
  226.6 0.9 constant_dynamic-slice_fusion.2
  227.5 1.7 fusion.44
  229.5 1.3 dynamic_update_slice.35
  230.8 0.9 constant_dynamic-slice_fusion.2
  231.8 1.7 fusion.44
  233.7 1.3 dynamic_update_slice.35
  235.0 0.9 constant_dynamic-slice_fusion.2
  236.0 1.7 fusion.44
  237.9 1.3 dynamic_update_slice.35
  239.2 40.9 %pmax.22 = f32[1664]{0:T(1024)S(1)} all-reduce(f32[1664]{0:T(1024)S(1)} %bitcast.126), channel_id=1, replica_groups=mesh['src'=16,'tgt'=16] {'src'}, use_global_device_ids=true, to_apply=%region_14.15 | all-reduce | flops 1664 | bytes 13312 | tf_op jit(solution)/shard_map/pmax | solution.py:71
  280.9 24.2 %psum.15 = f32[1664]{0:T(1024)S(1)} all-reduce(f32[1664]{0:T(1024)S(1)} %bitcast_multiply_fusion.2), channel_id=1, replica_groups=mesh['src'=16,'tgt'=16] {'src'}, use_global_device_ids=true, to_apply=%region_15.16 | all-reduce | flops 1664 | bytes 13312 | tf_op jit(solution)/shard_map/psum | solution.py:72
  305.7 21.1 %while.40 = (s32[]{:T(128)}, f32[2,512]{1,0:T(2,128)S(1)}, f32[2,512]{1,0:T(2,128)S(1)}, f32[2,32,512]{2,1,0:T(8,128)}, f32[1664]{0:T(1024)}, /*index=5*/f32[2,3...) while((s32[]{:T(128)}, f32[2,512]{1,0:T(2,128)S(1)}, ...), condition=%wide.region_20.21_spmd, body=%wide.region_16.20_spmd.sunk | while | flops 662862336 | bytes 10886793 | solution.py:46
  305.8 4.6 %fusion.48 = (f32[512]{0:T(512)S(1)}, f32[512,1664]{1,0:T(8,128)S(1)}) fusion(f32[1664]{0:T(1024)} %get-tuple-element.539, f32[32,1664]{1,0:T(8,128)} %get-tuple-element.538, f32[2,32,512]{2,1,0:T(8,128)S(1)} %get-tuple-element.536, s32[]{:T(128)S(6)} %copy.68, f32[1664]{0:T(1024)} %get-tuple-element.537, f32[512]{0:T(512)S(1)} %fusion.47, ...), kind=kOutput, calls=%fused_computation.39.clone.1 | convolution fusion | flops 333118976 | bytes 3710468 | tf_op jit(solution)/shard_map/while/body/eval_jaxpr/dot_general | solution.py:13
  311.1 5.2 %fusion.50 = f32[2,32,512]{2,1,0:T(8,128)} fusion(f32[2,32,512]{2,1,0:T(8,128)} %get-tuple-element.523, s32[]{:T(128)S(6)} %copy.68, f32[32,1664]{1,0:T(8,128)} %get-tuple-element.538, f32[512,1664]{1,0:T(8,128)S(1)} %get-tuple-element.448, f32[512]{0:T(512)S(1)} %get-tuple-element.447), kind=kOutput, calls=%fused_computation.21.clone.1 | convolution fusion | flops 328007680 | bytes 3688452 | tf_op jit(solution)/shard_map/while/body/eval_jaxpr/dot_general | solution.py:36
  316.3 4.6 %fusion.48 = (f32[512]{0:T(512)S(1)}, f32[512,1664]{1,0:T(8,128)S(1)}) fusion(f32[1664]{0:T(1024)} %get-tuple-element.539, f32[32,1664]{1,0:T(8,128)} %get-tuple-element.538, f32[2,32,512]{2,1,0:T(8,128)S(1)} %get-tuple-element.536, s32[]{:T(128)S(6)} %copy.68, f32[1664]{0:T(1024)} %get-tuple-element.537, f32[512]{0:T(512)S(1)} %fusion.47, ...), kind=kOutput, calls=%fused_computation.39.clone.1 | convolution fusion | flops 333118976 | bytes 3710468 | tf_op jit(solution)/shard_map/while/body/eval_jaxpr/dot_general | solution.py:13
  321.6 5.2 %fusion.50 = f32[2,32,512]{2,1,0:T(8,128)} fusion(f32[2,32,512]{2,1,0:T(8,128)} %get-tuple-element.523, s32[]{:T(128)S(6)} %copy.68, f32[32,1664]{1,0:T(8,128)} %get-tuple-element.538, f32[512,1664]{1,0:T(8,128)S(1)} %get-tuple-element.448, f32[512]{0:T(512)S(1)} %get-tuple-element.447), kind=kOutput, calls=%fused_computation.21.clone.1 | convolution fusion | flops 328007680 | bytes 3688452 | tf_op jit(solution)/shard_map/while/body/eval_jaxpr/dot_general | solution.py:36
  327.8 30.2 %pmax.23 = f32[1024]{0:T(1024)S(1)} all-reduce(f32[1024]{0:T(1024)S(1)} %bitcast.121), channel_id=1, replica_groups=mesh['src'=16,'tgt'=16] {'tgt'}, use_global_device_ids=true, to_apply=%region_21.22 | all-reduce | flops 1024 | bytes 8192 | tf_op jit(solution)/shard_map/pmax | solution.py:80
  358.0 1.0 copy.28
  359.1 1.3 dynamic_slice.17
  360.3 1.3 dynamic_slice.18
  362.2 28.5 %all-reduce.3 = f32[1024]{0:T(1024)S(1)} all-reduce(f32[1024]{0:T(1024)S(1)} %get-tuple-element.274), channel_id=3, replica_groups=mesh['src'=16,'tgt'=16] {'tgt'}, use_global_device_ids=true, to_apply=%region_23.24.clone | all-reduce | flops 1024 | bytes 8192
  390.8 46.9 %reduce-scatter.4.cloned.1.call-done = f32[64,32]{1,0:T(8,128)} async-done(((f32[1024,32]{1,0:T(8,128)}), f32[64,32]{1,0:T(8,128)}) %reduce-scatter.4.cloned.1.call-update) | async-done | bytes 8208
  (102 shorter events, 20.6 us)
Async XLA Ops:
  7.2 51.8 %copy-start.4 = (u32[256]{0:T(256)S(1)}, u32[256]{0:T(256)}, u32[]{:S(2)}) copy-start(u32[256]{0:T(256)} %constant.89) | copy-start | bytes 3076
  7.2 53.1 %copy-start.2 = (f32[104]{0:T(128)S(1)}, f32[104]{0:T(128)}, u32[]{:S(2)}) copy-start(f32[104]{0:T(128)} %param.13) | copy-start | bytes 1252
  7.2 53.4 %copy-start.3 = (f32[104]{0:T(128)S(1)}, f32[104]{0:T(128)}, u32[]{:S(2)}) copy-start(f32[104]{0:T(128)} %param.15) | copy-start | bytes 1252
  7.2 430.5 %reduce-scatter.4.cloned.1.call-start = ((), (), s32[]{:S(2)}) async-start(), calls=%async_computation.1 | async-start | bytes 557056
  27.3 0.8 copy-start
  239.2 66.5 %copy-start.1 = (f32[1024]{0:T(1024)}, f32[1024]{0:T(1024)S(1)}, u32[]{:S(2)}) copy-start(f32[1024]{0:T(1024)S(1)} %get-tuple-element.549) | copy-start | bytes 12292
Sparse Core Ops, SparseCore 0:
  359.2 78.4 reduce-scatter.3
where the time goes:
time: 448 us; the launch traced here: 446 us
  blocking collectives  273 us (61%)
  matrix products  51 us (11%)
  local copies, waits for them, and re-layouts  49.1 us (11%)
  waiting for transfers between devices  46.9 us (10%)
  between operations  16.1 us (4%)
  other arithmetic  9.89 us (2%)
    unnamed x2, blocking collectives  71.1 us
    unnamed x2, waiting for transfers between devices  46.9 us
    pmax x1, blocking collectives, body(): col_highest = lax.pmax(col_top, 'src')  40.9 us
    dot_general x17, matrix products, cost_scores(): lax.dot_general(row_cells, col_cells, (((0,), (0,)), ((), ())), precision...  40.6 us
    pmax x1, blocking collectives, body(): highest = lax.pmax(row_top, 'tgt')  31 us
    pmax x1, blocking collectives, body(): proj_highest = lax.pmax(proj_top, 'tgt')  30.2 us
    psum x1, blocking collectives, body(): row_totals = lax.psum(row_totals * jnp.exp(row_top - highest), 'tgt')  29 us
    all_gather x1, blocking collectives, body(): lax.all_gather(target, 'src', axis=1, tiled=True)  26.6 us
  transfers between devices with their start and end apart: 1, of which 1 were waited for; matrix products, arithmetic and copies ran while one was open for 1% of the time, Pallas kernels for 0%

commit v1 on v0

v1 whole, which is shorter than its diff:
```python
import math

import jax
import jax.numpy as jnp
from jax import lax
from jax.experimental import pallas as pl
from jax.experimental.pallas import tpu as pltpu
from jax.sharding import PartitionSpec as P

EPSILON = 0.05
LOG2E = 1.0 / math.log(2.0)
SCALE = LOG2E / EPSILON
F32 = jnp.float32
BF16 = jnp.bfloat16
MESH = pl.DeviceIdType.MESH
GROUP = 16
ROWS = 1024
COLS = 1664
OWN_ROWS = 64
OWN_COLS = 104
DIM = 32


def dot(a, b):
    return lax.dot_general(a, b, (((1,), (0,)), ((), ())), preferred_element_type=F32)


def split3(x):
    one = x.astype(BF16).astype(F32)
    rest = x - one
    two = rest.astype(BF16).astype(F32)
    return one, two, rest - two


def lane_iota(rows):
    return lax.broadcasted_iota(jnp.int32, (rows, 128), 1)


def sub_iota(rows):
    return lax.broadcasted_iota(jnp.int32, (rows, 128), 0)


def bias_rows(bias):
    one, two, three = split3(bias)
    sub = sub_iota(8)
    return jnp.where(sub == 0, one, jnp.where(sub == 1, two, jnp.where(sub == 2, three, 0.0)))


def combine(parts):
    top = parts[0]
    for part in parts[1:]:
        top = jnp.maximum(top, part)
    total = jnp.exp2(parts[0] - top)
    for part in parts[1:]:
        total = total + jnp.exp2(part - top)
    return top + jnp.log(total) * LOG2E


def column_pieces(block):
    start, pieces = block * 128, []
    while start < block * 128 + 128:
        shard, offset = divmod(start, OWN_COLS)
        stop = min((shard + 1) * OWN_COLS, block * 128 + 128)
        pieces.append((shard, offset, start - block * 128, stop - block * 128))
        start = stop
    return pieces


def kernel(
    src_ref, tgt_ref, pot_ref, slw_ref, tlw_ref,
    f_ref, g_ref, p_ref,
    pad, smsg, tmsg, srecv, trecv,
    xr, yr, xt, yt, tl,
    slw, tlw, lsend, lrecv, gsend, grecv, msend, mrecv, lall, gall,
    s_send, s_recv, t_send, t_recv, l_send, l_recv, g_send, g_recv, m_send, m_recv,
):
    me_t = lax.axis_index("tgt")
    me_s = lax.axis_index("src")

    def peer_t(k):
        return lax.rem(me_t + k, GROUP)

    def peer_s(k):
        return lax.rem(me_s + k, GROUP)

    barrier = pltpu.get_barrier_semaphore()

    def greet(k, carry):
        pl.semaphore_signal(barrier, inc=1, device_id={"tgt": peer_t(k)}, device_id_type=MESH)
        pl.semaphore_signal(barrier, inc=1, device_id={"src": peer_s(k)}, device_id_type=MESH)
        return carry

    lax.fori_loop(1, GROUP, greet, 0)

    pad[...] = jnp.zeros_like(pad)
    pad[0:DIM, 0:OWN_ROWS] = src_ref[...]
    pad[DIM : DIM + 1, 0:OWN_ROWS] = slw_ref[...] * LOG2E
    own = pad[...]
    src_sq = jnp.sum(own[0:DIM] * own[0:DIM], 0, keepdims=True)
    low = lane_iota(16) < 64
    smsg[0:16, :] = jnp.where(low, own[0:16], pltpu.roll(own[16:32], 64, 1))
    smsg[16:24, :] = own[32:40]
    tmsg[...] = jnp.zeros_like(tmsg)
    tmsg[0:DIM, 0:OWN_COLS] = tgt_ref[...]
    own_t = tmsg[0:DIM, :]
    tgt_sq = jnp.sum(own_t * own_t, 0, keepdims=True)
    tmsg[DIM : DIM + 1, 0:OWN_COLS] = (
        SCALE * (pot_ref[...] - tgt_sq[:, 0:OWN_COLS]) + LOG2E * tlw_ref[...]
    )
    tmsg[DIM + 1 : DIM + 2, 0:OWN_COLS] = LOG2E * tlw_ref[...]

    pl.semaphore_wait(barrier, 2 * (GROUP - 1))

    def over_t(src_at, dst, send, recv, k):
        return pltpu.make_async_remote_copy(
            src_ref=src_at, dst_ref=dst.at[me_t], send_sem=send.at[k], recv_sem=recv.at[me_t],
            device_id={"tgt": peer_t(k)}, device_id_type=MESH,
        )

    def over_s(src_at, dst, send, recv, k):
        return pltpu.make_async_remote_copy(
            src_ref=src_at, dst_ref=dst.at[me_s], send_sem=send.at[k], recv_sem=recv.at[me_s],
            device_id={"src": peer_s(k)}, device_id_type=MESH,
        )

    def wait_arrivals(dst, recv, peer):
        def one(k, carry):
            other = peer(k)
            pltpu.make_async_copy(dst.at[other], dst.at[other], recv.at[other]).wait()
            return carry

        lax.fori_loop(1, GROUP, one, 0)

    def loop(step):
        def one(k, carry):
            step(k)
            return carry

        lax.fori_loop(1, GROUP, one, 0)

    def send_cells(k):
        over_s(tmsg, trecv, t_send, t_recv, k).start()
        over_t(smsg, srecv, s_send, s_recv, k).start()

    loop(send_cells)
    srecv[me_t] = smsg[...]
    trecv[me_s] = tmsg[...]

    wait_arrivals(srecv, s_recv, peer_t)
    ones16 = jnp.where(sub_iota(16) < 3, 1.0, 0.0).astype(BF16)
    zeros48 = jnp.zeros((48, 128), BF16)
    zeros56 = jnp.zeros((56, 128), F32)
    for p in range(8):
        a, b = srecv[2 * p], srecv[2 * p + 1]
        first = jnp.where(low, a[0:16], pltpu.roll(b[0:16], 64, 1))
        second = jnp.where(low, pltpu.roll(a[0:16], 64, 1), b[0:16])
        x = jnp.concatenate([first, second], 0) * (2.0 * SCALE)
        x1, x2, x3 = split3(x)
        at = slice(128 * p, 128 * p + 128)
        slw[p : p + 1, :] = jnp.where(low[0:1], a[16:17], pltpu.roll(b[16:24], 64, 1)[0:1])
        top = jnp.concatenate([x1, x1, x2, x2], 0)
        end = jnp.concatenate([x1, x3], 0)
        xr[0:128, at] = top.astype(BF16)
        xr[128:192, at] = end.astype(BF16)
        xr[192:208, at] = ones16
        xr[208:256, at] = zeros48
        xt[at, 0:128] = jnp.transpose(top).astype(BF16)

    wait_arrivals(trecv, t_recv, peer_s)
    for q in range(13):
        at = slice(128 * q, 128 * q + 128)
        lane = lane_iota(40)
        block = None
        for shard, offset, start, stop in column_pieces(q):
            piece = trecv[shard]
            shift = (start - offset) % 128
            if shift:
                piece = pltpu.roll(piece, shift, 1)
            block = piece if block is None else jnp.where(lane >= start, piece, block)
        y1, y2, y3 = split3(block[0:DIM])
        tlw[q : q + 1, :] = block[DIM + 1 : DIM + 2]
        top = jnp.concatenate([y1, y2, y1, y2], 0)
        end = jnp.concatenate([y3, y1], 0)
        yr[0:128, at] = top.astype(BF16)
        yr[128:192, at] = end.astype(BF16)
        yr[192:208, at] = ones16
        yr[208:256, at] = zeros48
        tl[0:64, at] = yr[0:64, at]
        tl[64:96, at] = yr[128:160, at]
        tl[96:112, at] = jnp.ones((16, 128), BF16)
        yt[at, 0:128] = jnp.transpose(top).astype(BF16)
        tail = jnp.concatenate([end, bias_rows(block[DIM : DIM + 1]), zeros56], 0)
        yt[at, 128:256] = jnp.transpose(tail).astype(BF16)

    for n in range(4):
        scores = dot(yt[...], xr[:, 256 * n : 256 * n + 256])
        top = jnp.max(scores, 0, keepdims=True)
        part = top + jnp.log(jnp.sum(jnp.exp2(scores - top), 0, keepdims=True)) * LOG2E
        lsend[2 * n : 2 * n + 1, :] = part[:, 0:128]
        lsend[2 * n + 1 : 2 * n + 2, :] = part[:, 128:256]
    loop(lambda k: over_t(lsend, lrecv, l_send, l_recv, k).start())
    lrecv[me_t] = lsend[...]
    wait_arrivals(lrecv, l_recv, peer_t)
    row_lse = combine([lrecv[k] for k in range(GROUP)])
    lall[...] = row_lse
    for p in range(8):
        at = slice(128 * p, 128 * p + 128)
        bias = slw[p : p + 1, :] - row_lse[p : p + 1, :]
        tail = jnp.concatenate([xr[128:192, at].astype(F32), bias_rows(bias), zeros56], 0)
        xt[at, 128:256] = jnp.transpose(tail).astype(BF16)

    for n in range(7):
        width = 256 if n < 6 else 128
        scores = dot(xt[...], yr[:, 256 * n : 256 * n + width])
        top = jnp.max(scores, 0, keepdims=True)
        part = top + jnp.log(jnp.sum(jnp.exp2(scores - top), 0, keepdims=True)) * LOG2E
        for h in range(width // 128):
            gsend[2 * n + h : 2 * n + h + 1, :] = part[:, 128 * h : 128 * h + 128]
    gsend[13:16, :] = jnp.zeros((3, 128), F32)
    loop(lambda k: over_s(gsend, grecv, g_send, g_recv, k).start())
    grecv[me_s] = gsend[...]

    row = lall[pl.ds(me_t // 2, 1), :]
    row = jnp.where(lax.rem(me_t, 2) == 1, pltpu.roll(row, 64, 1), row)
    f_ref[...] = (src_sq - (EPSILON / LOG2E) * row)[:, 0:OWN_ROWS]

    wait_arrivals(grecv, g_recv, peer_s)
    col_lse = combine([grecv[k] for k in range(GROUP)])
    gall[...] = col_lse
    for q in range(13):
        at = slice(128 * q, 128 * q + 128)
        bias = tlw[q : q + 1, :] - col_lse[q : q + 1, :]
        tail = jnp.concatenate([yr[128:192, at].astype(F32), bias_rows(bias), zeros56], 0)
        yt[at, 128:256] = jnp.transpose(tail).astype(BF16)

    low40 = lane_iota(40) < 64
    for n in range(4):
        scores = dot(yt[...], xr[:, 256 * n : 256 * n + 256])
        top = jnp.max(scores, 0, keepdims=True)
        weights = jnp.exp2(scores - top)
        high = weights.astype(BF16)
        rest = (weights - high.astype(F32)).astype(BF16)
        moments = dot(tl[...], high) + dot(tl[...], rest)
        message = jnp.concatenate(
            [
                moments[0:32] + moments[32:64] + moments[64:96],
                jnp.where(lax.broadcasted_iota(jnp.int32, (8, 256), 0) == 0, moments[96:104], top),
            ],
            0,
        )
        for h in range(2):
            half = message[:, 128 * h : 128 * h + 128]
            msend[4 * n + 2 * h] = half
            msend[4 * n + 2 * h + 1] = pltpu.roll(half, 64, 1)
    loop(lambda k: over_t(msend.at[peer_t(k)], mrecv, m_send, m_recv, k).start())
    mrecv[me_t] = msend[me_t]

    start = me_s * OWN_COLS
    line, offset = start // 128, lax.rem(start, 128)
    here = pltpu.roll(gall[pl.ds(line, 1), :], 128 - offset, 1)
    after = pltpu.roll(gall[pl.ds(line + 1, 1), :], 128 - offset, 1)
    col = jnp.where(lane_iota(1) < 128 - offset, here, after)
    g_ref[...] = (tgt_sq - (EPSILON / LOG2E) * col)[:, 0:OWN_COLS]

    wait_arrivals(mrecv, m_recv, peer_t)
    parts = [mrecv[k] for k in range(GROUP)]
    top = parts[0][33:34]
    for part in parts[1:]:
        top = jnp.maximum(top, part[33:34])
    total = jnp.zeros((40, 128), F32)
    for part in parts:
        total = total + part * jnp.exp2(part[33:34] - top)
    p_ref[...] = (total[0:32] / total[32:33])[:, 0:OWN_ROWS]

    def finish(k):
        over_s(tmsg, trecv, t_send, t_recv, k).wait_send()
        over_t(smsg, srecv, s_send, s_recv, k).wait_send()
        over_t(lsend, lrecv, l_send, l_recv, k).wait_send()
        over_s(gsend, grecv, g_send, g_recv, k).wait_send()
        over_t(msend.at[peer_t(k)], mrecv, m_send, m_recv, k).wait_send()

    loop(finish)


def body(source, target, target_pot, source_logw, target_logw):
    vmem = pl.BlockSpec(memory_space=pltpu.VMEM)
    f_new, g_new, projection = pl.pallas_call(
        kernel,
        out_shape=(
            jax.ShapeDtypeStruct((1, OWN_ROWS), F32),
            jax.ShapeDtypeStruct((1, OWN_COLS), F32),
            jax.ShapeDtypeStruct((DIM, OWN_ROWS), F32),
        ),
        in_specs=[vmem] * 5,
        out_specs=(vmem,) * 3,
        scratch_shapes=[
            pltpu.VMEM((40, 128), F32),
            pltpu.VMEM((24, 128), F32),
            pltpu.VMEM((40, 128), F32),
            pltpu.VMEM((GROUP, 24, 128), F32),
            pltpu.VMEM((GROUP, 40, 128), F32),
            pltpu.VMEM((256, ROWS), BF16),
            pltpu.VMEM((256, COLS), BF16),
            pltpu.VMEM((ROWS, 256), BF16),
            pltpu.VMEM((COLS, 256), BF16),
            pltpu.VMEM((112, COLS), BF16),
            pltpu.VMEM((8, 128), F32),
            pltpu.VMEM((16, 128), F32),
            pltpu.VMEM((8, 128), F32),
            pltpu.VMEM((GROUP, 8, 128), F32),
            pltpu.VMEM((16, 128), F32),
            pltpu.VMEM((GROUP, 16, 128), F32),
            pltpu.VMEM((GROUP, 40, 128), F32),
            pltpu.VMEM((GROUP, 40, 128), F32),
            pltpu.VMEM((8, 128), F32),
            pltpu.VMEM((16, 128), F32),
        ]
        + [pltpu.SemaphoreType.DMA((GROUP,))] * 10,
        compiler_params=pltpu.CompilerParams(
            collective_id=0, has_side_effects=True, vmem_limit_bytes=60 * 1024 * 1024
        ),
    )(
        source,
        target,
        target_pot.reshape(1, OWN_COLS),
        source_logw.reshape(1, OWN_ROWS),
        target_logw.reshape(1, OWN_COLS),
    )
    return f_new.reshape(OWN_ROWS), g_new.reshape(OWN_COLS), projection


def solution(mesh):
    return jax.shard_map(
        body,
        mesh=mesh,
        in_specs=(
            P(None, ("src", "tgt")),
            P(None, ("tgt", "src")),
            P(("tgt", "src")),
            P(("src", "tgt")),
            P(("tgt", "src")),
        ),
        out_specs=(P(("src", "tgt")), P(("tgt", "src")), P(None, ("src", "tgt"))),
        check_vma=False,
    )
```

time: 448 us -> 52.7 us (0.12)
  blocking collectives: 273 us -> 0 us
  matrix products: 51 us -> 0 us
  Pallas kernels: 0 us -> 48.7 us
  waiting for transfers between devices: 46.9 us -> 0 us
  local copies, waits for them, and re-layouts: 49.1 us -> 3.07 us
  between operations: 16.1 us -> 0.65 us
  other arithmetic: 9.89 us -> 0 us
    pmax x3 -> x0, blocking collectives: 102 us -> none  [the longest x1 40.9 us: body(): col_highest = lax.pmax(col_top, 'src')]
    unnamed x2 -> x0, blocking collectives: 71.1 us -> none
    psum x2 -> x0, blocking collectives: 53.2 us -> none  [the longest x1 29 us: body(): row_totals = lax.psum(row_totals * jnp.exp(row_top - highest), 'tgt')]
    dot_general x19 -> x0, matrix products: 51 us -> none  [the longest x17 40.6 us: cost_scores(): lax.dot_general(row_cells, col_cells, (((0,), (0,)), ((), ())), precision...]
    pallas_call x0 -> x1, Pallas kernels: none -> 48.7 us  [body(): pl.pallas_call(kernel, out_shape=(jax.ShapeDtypeStruct((1, OWN_ROWS), F32...]
    unnamed x2 -> x0, waiting for transfers between devices: 46.9 us -> none
    all_gather x2 -> x0, blocking collectives: 46.3 us -> none  [the longest x1 26.6 us: body(): lax.all_gather(target, 'src', axis=1, tiled=True)]
    dynamic_update_slice x34 -> x0, local copies, waits for them, and re-layouts: 22.7 us -> none  [log_sums(): result = lax.map(one_block, blocks)]
  transfers between devices with their start and end apart: 1 -> 0, of which waited for: 1 -> 0; matrix products, arithmetic and copies ran while one was open for 1% -> 0% of each run, Pallas kernels for 0% -> 0%
where the time goes in v1:
time: 52.7 us; the launch traced here: 52.4 us
  Pallas kernels  48.7 us (92%)
  local copies, waits for them, and re-layouts  3.07 us (6%)
  between operations  0.65 us (1%)
    pallas_call x1, Pallas kernels, body(): pl.pallas_call(kernel, out_shape=(jax.ShapeDtypeStruct((1, OWN_ROWS), F32...  48.7 us
    unnamed x7, local copies, waits for them, and re-layouts  3.07 us

profile of v1, /device:TPU:1, one launch (start us, length us, event | category | flops | bytes accessed | tf_op | source)
XLA Modules:
  0.0 52.4 jit_solution(7248450108413421152)
XLA Ops:
  0.6 48.7 %shard_map.76 = (f32[1,64]{1,0:T(1,128)}, f32[1,104]{1,0:T(1,128)}, f32[32,64]{1,0:T(8,128)}) custom-call(f32[32,64]{1,0:T(8,128)} %src_ref.1, f32[32,104]{1,0:T(8,128)} %tgt_ref.1, f32[1,104]{1,0:T(1,128)} %bitcast.5, f32[1,64]{1,0:T(1,128)} %bitcast.6, f32[1,104]{1,0:T(1,128)} %bitcast.7), custom_call_target="tpu_custom_call" | custom-call | tf_op jit(solution)/shard_map/pallas_call | solution.py:287
  49.4 0.0 copy-start.1
  49.4 0.6 %copy-done.1 = f32[1,64]{1,0:T(1,128)S(1)} copy-done((f32[1,64]{1,0:T(1,128)S(1)}, f32[1,64]{1,0:T(1,128)}, u32[]{:S(2)}) %copy-start.1) | copy-done | bytes 280
  50.0 0.0 copy-start
  50.0 0.5 copy.11
  50.5 0.1 copy-done
  50.6 0.5 copy.12
  51.1 1.3 %copy.13 = f32[32,64]{1,0:T(8,128)} copy(f32[32,64]{1,0:T(8,128)} %get-tuple-element.14) | data formatting | bytes 16384
Async XLA Ops:
  49.4 0.6 %copy-start.1 = (f32[1,64]{1,0:T(1,128)S(1)}, f32[1,64]{1,0:T(1,128)}, u32[]{:S(2)}) copy-start(f32[1,64]{1,0:T(1,128)} %get-tuple-element.6) | copy-start | bytes 772
  50.0 0.6 %copy-start = (f32[1,104]{1,0:T(1,128)S(1)}, f32[1,104]{1,0:T(1,128)}, u32[]{:S(2)}) copy-start(f32[1,104]{1,0:T(1,128)} %get-tuple-element.7) | copy-start | bytes 1252

commit v2 on v1

v2 whole, which is shorter than its diff:
```python
import math

import jax
import jax.numpy as jnp
from jax import lax
from jax.experimental import pallas as pl
from jax.experimental.pallas import tpu as pltpu
from jax.sharding import PartitionSpec as P

EPSILON = 0.05
LOG2E = 1.0 / math.log(2.0)
SCALE = LOG2E / EPSILON
F32 = jnp.float32
BF16 = jnp.bfloat16
MESH = pl.DeviceIdType.MESH
GROUP = 16
ROWS = 1024
COLS = 1664
OWN_ROWS = 64
OWN_COLS = 104
DIM = 32
SRC_LINES = 17
TGT_LINES = 34
HALVES = ((0, 1024), (1024, 640))


def ring(d, n):
    return min(d, n - d)


TGT_PEERS = sorted(
    [(y, x) for y in range(4) for x in range(4) if y or x],
    key=lambda o: -(ring(o[0], 4) + ring(o[1], 4)),
)
SRC_PEERS = sorted(
    [(z, c) for z in range(8) for c in range(2) if z or c],
    key=lambda o: (-ring(o[0], 8), o[1]),
)
Z_PEERS = (4, 3, 5, 2, 6, 1, 7)
Z_ARRIVALS = (1, 7, 2, 6, 3, 5, 4)


def dot(a, b):
    return lax.dot_general(a, b, (((1,), (0,)), ((), ())), preferred_element_type=F32)


def split3(x):
    one = x.astype(BF16).astype(F32)
    rest = x - one
    two = rest.astype(BF16).astype(F32)
    return one, two, rest - two


def lane_iota(rows):
    return lax.broadcasted_iota(jnp.int32, (rows, 128), 1)


def sub_iota(rows):
    return lax.broadcasted_iota(jnp.int32, (rows, 128), 0)


def bias_rows(bias):
    one, two, three = split3(bias)
    sub = sub_iota(8)
    return jnp.where(sub == 0, one, jnp.where(sub == 1, two, jnp.where(sub == 2, three, 0.0)))


def combine(parts):
    top = parts[0]
    for part in parts[1:]:
        top = jnp.maximum(top, part)
    total = jnp.exp2(parts[0] - top)
    for part in parts[1:]:
        total = total + jnp.exp2(part - top)
    return top + jnp.log(total) * LOG2E


def column_pieces(block):
    start, pieces = block * 128, []
    while start < block * 128 + 128:
        shard, offset = divmod(start, OWN_COLS)
        stop = min((shard + 1) * OWN_COLS, block * 128 + 128)
        pieces.append((shard, offset, start - block * 128, stop - block * 128))
        start = stop
    return pieces


def lse(scores):
    top = jnp.max(scores, 0, keepdims=True)
    return top + jnp.log(jnp.sum(jnp.exp2(scores - top), 0, keepdims=True)) * LOG2E


def kernel(
    src_hbm, tgt_hbm, pot_hbm, slw_hbm, tlw_hbm,
    f_ref, g_ref, p_ref,
    src_v, tgt_v, pot_v, slw_v, tlw_v,
    pad, smsg, tmsg, srecv, trecv,
    xr, yr, xt, yt, tl,
    slw, tlw, lpart, lsend, lrecv, gsend, grecv, moms, tops, msend, mrecv, lall, gall,
    in_sem, s_send, s_recv, t_send, t_recv, l_send, l_recv, g_send, g_recv, m_send, m_recv,
):
    me_t = lax.axis_index("tgt")
    me_s = lax.axis_index("src")
    me_y, me_x = me_t // 4, lax.rem(me_t, 4)
    me_z, me_c = me_s // 2, lax.rem(me_s, 2)

    def at_t(offset):
        return lax.rem(me_y + offset[0], 4) * 4 + lax.rem(me_x + offset[1], 4)

    def at_s(offset):
        return lax.rem(me_z + offset[0], 8) * 2 + lax.rem(me_c + offset[1], 2)

    barrier = pltpu.get_barrier_semaphore()
    for offset in TGT_PEERS:
        pl.semaphore_signal(barrier, inc=1, device_id={"tgt": at_t(offset)}, device_id_type=MESH)
    for offset in SRC_PEERS:
        pl.semaphore_signal(barrier, inc=1, device_id={"src": at_s(offset)}, device_id_type=MESH)

    inputs = [
        pltpu.make_async_copy(a, b, in_sem.at[n])
        for n, (a, b) in enumerate(
            ((src_hbm, src_v), (slw_hbm, slw_v), (tgt_hbm, tgt_v), (pot_hbm, pot_v), (tlw_hbm, tlw_v))
        )
    ]
    for copy in inputs:
        copy.start()
    pad[...] = jnp.zeros_like(pad)
    tmsg[...] = jnp.zeros_like(tmsg)
    low = lane_iota(16) < 64
    for copy in inputs:
        copy.wait()

    pad[0:DIM, 0:OWN_ROWS] = src_v[...]
    pad[DIM : DIM + 1, 0:OWN_ROWS] = slw_v[...] * LOG2E
    own = pad[...]
    src_sq = jnp.sum(own[0:DIM] * own[0:DIM], 0, keepdims=True)
    smsg[0:16, :] = jnp.where(low, own[0:16], pltpu.roll(own[16:32], 64, 1))
    smsg[16:24, :] = own[32:40]
    tmsg[0:DIM, 0:OWN_COLS] = tgt_v[...]
    own_t = tmsg[0:DIM, :]
    tgt_sq = jnp.sum(own_t * own_t, 0, keepdims=True)
    tmsg[DIM : DIM + 1, 0:OWN_COLS] = (
        SCALE * (pot_v[...] - tgt_sq[:, 0:OWN_COLS]) + LOG2E * tlw_v[...]
    )
    tmsg[DIM + 1 : DIM + 2, 0:OWN_COLS] = LOG2E * tlw_v[...]

    pl.semaphore_wait(barrier, 2 * (GROUP - 1))
    sent = []

    def to_t(offset, src, dst, send, recv):
        copy = pltpu.make_async_remote_copy(
            src_ref=src, dst_ref=dst, send_sem=send, recv_sem=recv.at[me_t],
            device_id={"tgt": at_t(offset)}, device_id_type=MESH,
        )
        copy.start()
        sent.append(copy)

    def to_s(offset, slot, src, dst, send, recv):
        copy = pltpu.make_async_remote_copy(
            src_ref=src, dst_ref=dst, send_sem=send, recv_sem=recv.at[slot],
            device_id={"src": at_s(offset)}, device_id_type=MESH,
        )
        copy.start()
        sent.append(copy)

    def arrive(dst, sem):
        pltpu.make_async_copy(dst, dst, sem).wait()

    tgt_own = tmsg.at[0:TGT_LINES]
    for n, z in enumerate(Z_PEERS):
        to_s((z, 0), me_s, tgt_own, trecv.at[me_s, 0:TGT_LINES], t_send.at[n], t_recv)
    to_s((0, 1), me_s, tgt_own, trecv.at[me_s, 0:TGT_LINES], t_send.at[7], t_recv)
    src_own = smsg.at[0:SRC_LINES]
    for n, offset in enumerate(TGT_PEERS):
        to_t(offset, src_own, srecv.at[me_t, 0:SRC_LINES], s_send.at[n], s_recv)
    srecv[me_t] = smsg[...]
    trecv[me_s] = tmsg[...]
    ones16 = jnp.where(sub_iota(16) < 3, 1.0, 0.0).astype(BF16)
    zeros48 = jnp.zeros((48, 128), BF16)
    zeros56 = jnp.zeros((56, 128), F32)

    for offset in reversed(TGT_PEERS):
        slot = at_t(offset)
        arrive(srecv.at[slot, 0:SRC_LINES], s_recv.at[slot])
    for p in range(8):
        a, b = srecv[2 * p], srecv[2 * p + 1]
        first = jnp.where(low, a[0:16], pltpu.roll(b[0:16], 64, 1))
        second = jnp.where(low, pltpu.roll(a[0:16], 64, 1), b[0:16])
        x1, x2, x3 = split3(jnp.concatenate([first, second], 0) * (2.0 * SCALE))
        at = slice(128 * p, 128 * p + 128)
        slw[p : p + 1, :] = jnp.where(low[0:1], a[16:17], pltpu.roll(b[16:24], 64, 1)[0:1])
        xr[0:128, at] = jnp.concatenate([x1, x1, x2, x2], 0).astype(BF16)
        xr[128:192, at] = jnp.concatenate([x1, x3], 0).astype(BF16)
        xr[192:208, at] = ones16
        xr[208:256, at] = zeros48

    def take(n, z):
        pair = lax.rem(me_z + z, 8)
        tops_t, tails_t = [], []
        for c in range(2):
            block = trecv[2 * pair + c]
            y1, y2, y3 = split3(block[0:DIM])
            tops_t.append(jnp.transpose(jnp.concatenate([y1, y2, y1, y2], 0))[0:OWN_COLS])
            tail = jnp.concatenate([y3, y1, bias_rows(block[DIM : DIM + 1]), zeros56], 0)
            tails_t.append(jnp.transpose(tail)[0:OWN_COLS])
        at = pl.ds(pl.multiple_of(pair * (2 * OWN_COLS), 16), 2 * OWN_COLS)
        yt[at, 0:128] = jnp.concatenate(tops_t, 0).astype(BF16)
        yt[at, 128:256] = jnp.concatenate(tails_t, 0).astype(BF16)
        part = lse(dot(yt[at, :], xr[...]))
        for p in range(8):
            lpart[n, p : p + 1, :] = part[:, 128 * p : 128 * p + 128]

    partner = lax.rem(me_c + 1, 2)
    arrive(trecv.at[me_z * 2 + partner, 0:TGT_LINES], t_recv.at[me_z * 2 + partner])
    for n in range(8):
        if n < 7:
            pair = lax.rem(me_z + Z_ARRIVALS[n], 8)
            slot = pair * 2 + me_c
            here = trecv.at[slot, 0:TGT_LINES]
            arrive(here, t_recv.at[slot])
            to_s((0, 1), slot, here, here, t_send.at[8 + n], t_recv)
        take(n, 0 if n == 0 else Z_ARRIVALS[n - 1])
        if n < 7:
            slot = pair * 2 + partner
            arrive(trecv.at[slot, 0:TGT_LINES], t_recv.at[slot])
    lsend[...] = combine([lpart[n] for n in range(8)])
    for n, offset in enumerate(TGT_PEERS):
        to_t(offset, lsend, lrecv.at[me_t], l_send.at[n], l_recv)
    lrecv[me_t] = lsend[...]

    for p in range(8):
        at = slice(128 * p, 128 * p + 128)
        xt[at, 0:128] = jnp.transpose(xr[0:128, at].astype(F32)).astype(BF16)
    for q in range(13):
        at = slice(128 * q, 128 * q + 128)
        lane = lane_iota(40)
        block = None
        for shard, offset, start, stop in column_pieces(q):
            piece = trecv[shard]
            shift = (start - offset) % 128
            if shift:
                piece = pltpu.roll(piece, shift, 1)
            block = piece if block is None else jnp.where(lane >= start, piece, block)
        y1, y2, y3 = split3(block[0:DIM])
        tlw[q : q + 1, :] = block[DIM + 1 : DIM + 2]
        yr[0:128, at] = jnp.concatenate([y1, y2, y1, y2], 0).astype(BF16)
        yr[128:192, at] = jnp.concatenate([y3, y1], 0).astype(BF16)
        yr[192:208, at] = ones16
        yr[208:256, at] = zeros48
        tl[0:32, at] = y1.astype(BF16)
        tl[32:48, at] = jnp.ones((16, 128), BF16)
        tl[48:80, at] = y2.astype(BF16)

    for offset in reversed(TGT_PEERS):
        slot = at_t(offset)
        arrive(lrecv.at[slot], l_recv.at[slot])
    row_lse = combine([lrecv[k] for k in range(GROUP)])
    lall[...] = row_lse
    for p in range(8):
        at = slice(128 * p, 128 * p + 128)
        bias = slw[p : p + 1, :] - row_lse[p : p + 1, :]
        tail = jnp.concatenate([xr[128:192, at].astype(F32), bias_rows(bias), zeros56], 0)
        xt[at, 128:256] = jnp.transpose(tail).astype(BF16)

    for half, (base, count) in enumerate(HALVES):
        for start in range(0, count, 256):
            width = min(256, count - start)
            part = lse(dot(xt[...], yr[:, base + start : base + start + width]))
            for h in range(width // 128):
                line = start // 128 + h
                gsend[half, line : line + 1, :] = part[:, 128 * h : 128 * h + 128]
        lines = count // 128
        for n, offset in enumerate(SRC_PEERS):
            to_s(offset, half * GROUP + me_s, gsend.at[half, 0:lines], grecv.at[half, me_s, 0:lines],
                 g_send.at[half * GROUP + n], g_recv)
    for half in range(2):
        grecv[half, me_s] = gsend[half]

    row = lall[pl.ds(me_y * 2 + me_x // 2, 1), :]
    row = jnp.where(lax.rem(me_t, 2) == 1, pltpu.roll(row, 64, 1), row)
    f_ref[...] = (src_sq - (EPSILON / LOG2E) * row)[:, 0:OWN_ROWS]

    for half, (base, count) in enumerate(HALVES):
        lines = count // 128
        for offset in reversed(SRC_PEERS):
            slot = at_s(offset)
            arrive(grecv.at[half, slot, 0:lines], g_recv.at[half * GROUP + slot])
        if half == 1:
            pass
        col_lse = combine([grecv[half, k] for k in range(GROUP)])
        gall[8 * half : 8 * half + 8, :] = col_lse
        for line in range(lines):
            at = slice(base + 128 * line, base + 128 * line + 128)
            q = base // 128 + line
            bias = tlw[q : q + 1, :] - col_lse[line : line + 1, :]
            tail = jnp.concatenate([yr[128:192, at].astype(F32), bias_rows(bias), zeros56], 0)
            yt[at, 128:256] = jnp.transpose(tail).astype(BF16)
        span = slice(base, base + count)
        for order in ((0, 1, 2, 3), (2, 1, 3, 0))[half]:
            tile = lax.rem(me_y + order, 4)
            columns = pl.ds(pl.multiple_of(tile * 256, 256), 256)
            scores = dot(yt[span, :], xr[:, columns])
            top = jnp.max(scores, 0, keepdims=True)
            weights = jnp.exp2(scores - top)
            high = weights.astype(BF16)
            rest = (weights - high.astype(F32)).astype(BF16)
            main = dot(tl[0:80, span], high)
            moments = jnp.concatenate(
                [main[0:32] + main[48:80], main[32:40]], 0
            ) + dot(tl[0:48, span], rest)[0:40]
            if half == 0:
                moms[order] = moments
                tops[order] = jnp.broadcast_to(top, (8, 256))
                continue
            before = tops[order]
            both = jnp.maximum(before, top)
            fix_a, fix_b = jnp.exp2(before - both), jnp.exp2(top - both)
            moments = moms[order] * fix_a[0:1] + moments * fix_b[0:1]
            for u in range(4):
                lanes = slice(128 * (u // 2), 128 * (u // 2) + 128)
                one, two = moments[0:16, lanes], moments[16:32, lanes]
                three, four = moments[32:40, lanes], both[:, lanes]
                if u % 2 == 0:
                    two, four = pltpu.roll(two, 64, 1), pltpu.roll(four, 64, 1)
                else:
                    one, three = pltpu.roll(one, 64, 1), pltpu.roll(three, 64, 1)
                msend[tile * 4 + u, 0:16, :] = jnp.where(low, one, two)
                msend[tile * 4 + u, 16:24, :] = jnp.where(low[0:8], three, four)
            for x in range(0 if order else 1, 4):
                slot = tile * 4 + lax.rem(me_x + x, 4)
                to_t((order, x), msend.at[slot, 0:SRC_LINES], mrecv.at[me_t, 0:SRC_LINES],
                     m_send.at[order * 4 + x], m_recv)
    mrecv[me_t] = msend[me_t]

    start = me_s * OWN_COLS
    line, offset = start // 128, lax.rem(start, 128)
    here = pltpu.roll(gall[pl.ds(line, 1), :], 128 - offset, 1)
    after = pltpu.roll(gall[pl.ds(line + 1, 1), :], 128 - offset, 1)
    col = jnp.where(lane_iota(1) < 128 - offset, here, after)
    g_ref[...] = (tgt_sq - (EPSILON / LOG2E) * col)[:, 0:OWN_COLS]

    for offset in reversed(TGT_PEERS):
        slot = at_t(offset)
        arrive(mrecv.at[slot, 0:SRC_LINES], m_recv.at[slot])
    top = mrecv[0, 16:17, :]
    for k in range(1, GROUP):
        top = jnp.maximum(top, mrecv[k, 16:17, :])
    acc, norm = jnp.zeros((16, 128), F32), jnp.zeros((1, 128), F32)
    low1 = low[0:1]
    for k in range(GROUP):
        last = mrecv[k, 16:17, :]
        fix = jnp.exp2(last - top)
        fix = jnp.where(low1, pltpu.roll(fix, 64, 1), fix)
        acc = acc + mrecv[k, 0:16, :] * fix
        norm = norm + last * fix
    ratio = acc / jnp.where(low1, norm, pltpu.roll(norm, 64, 1))
    p_ref[0:16, :] = ratio[:, 0:OWN_ROWS]
    p_ref[16:32, :] = pltpu.roll(ratio, 64, 1)[:, 0:OWN_ROWS]
    for copy in sent:
        copy.wait_send()


def body(source, target, target_pot, source_logw, target_logw):
    vmem = pl.BlockSpec(memory_space=pltpu.VMEM)
    f_new, g_new, projection = pl.pallas_call(
        kernel,
        out_shape=(
            jax.ShapeDtypeStruct((1, OWN_ROWS), F32),
            jax.ShapeDtypeStruct((1, OWN_COLS), F32),
            jax.ShapeDtypeStruct((DIM, OWN_ROWS), F32),
        ),
        in_specs=[pl.BlockSpec(memory_space=pl.ANY)] * 5,
        out_specs=(vmem,) * 3,
        scratch_shapes=[
            pltpu.VMEM((DIM, OWN_ROWS), F32),
            pltpu.VMEM((DIM, OWN_COLS), F32),
            pltpu.VMEM((1, OWN_COLS), F32),
            pltpu.VMEM((1, OWN_ROWS), F32),
            pltpu.VMEM((1, OWN_COLS), F32),
            pltpu.VMEM((40, 128), F32),
            pltpu.VMEM((24, 128), F32),
            pltpu.VMEM((40, 128), F32),
            pltpu.VMEM((GROUP, 24, 128), F32),
            pltpu.VMEM((GROUP, 40, 128), F32),
            pltpu.VMEM((256, ROWS), BF16),
            pltpu.VMEM((256, COLS), BF16),
            pltpu.VMEM((ROWS, 256), BF16),
            pltpu.VMEM((COLS, 256), BF16),
            pltpu.VMEM((80, COLS), BF16),
            pltpu.VMEM((8, 128), F32),
            pltpu.VMEM((16, 128), F32),
            pltpu.VMEM((8, 8, 128), F32),
            pltpu.VMEM((8, 128), F32),
            pltpu.VMEM((GROUP, 8, 128), F32),
            pltpu.VMEM((2, 8, 128), F32),
            pltpu.VMEM((2, GROUP, 8, 128), F32),
            pltpu.VMEM((4, 40, 256), F32),
            pltpu.VMEM((4, 8, 256), F32),
            pltpu.VMEM((GROUP, 24, 128), F32),
            pltpu.VMEM((GROUP, 24, 128), F32),
            pltpu.VMEM((8, 128), F32),
            pltpu.VMEM((16, 128), F32),
            pltpu.SemaphoreType.DMA((5,)),
        ]
        + [pltpu.SemaphoreType.DMA((GROUP,))] * 6
        + [pltpu.SemaphoreType.DMA((2 * GROUP,))] * 2
        + [pltpu.SemaphoreType.DMA((GROUP,))] * 2,
        compiler_params=pltpu.CompilerParams(
            collective_id=0, has_side_effects=True, vmem_limit_bytes=60 * 1024 * 1024
        ),
    )(
        source,
        target,
        target_pot.reshape(1, OWN_COLS),
        source_logw.reshape(1, OWN_ROWS),
        target_logw.reshape(1, OWN_COLS),
    )
    return f_new.reshape(OWN_ROWS), g_new.reshape(OWN_COLS), projection


def solution(mesh):
    return jax.shard_map(
        body,
        mesh=mesh,
        in_specs=(
            P(None, ("src", "tgt")),
            P(None, ("tgt", "src")),
            P(("tgt", "src")),
            P(("src", "tgt")),
            P(("tgt", "src")),
        ),
        out_specs=(P(("src", "tgt")), P(("tgt", "src")), P(None, ("src", "tgt"))),
        check_vma=False,
    )
```

time: 52.7 us -> 48.1 us (0.913)
  Pallas kernels: 48.7 us -> 44.1 us
    pallas_call x1, Pallas kernels: 48.7 us -> 44.1 us  [body(): pl.pallas_call(kernel, out_shape=(jax.ShapeDtypeStruct((1, OWN_ROWS), F32...]
where the time goes in v2:
time: 48.1 us; the launch traced here: 47.8 us
  Pallas kernels  44.1 us (92%)
  local copies, waits for them, and re-layouts  3.07 us (6%)
  between operations  0.65 us (1%)
    pallas_call x1, Pallas kernels, body(): pl.pallas_call(kernel, out_shape=(jax.ShapeDtypeStruct((1, OWN_ROWS), F32...  44.1 us
    unnamed x7, local copies, waits for them, and re-layouts  3.07 us

profile of v2, /device:TPU:1, one launch (start us, length us, event | category | flops | bytes accessed | tf_op | source)
XLA Modules:
  0.0 47.8 jit_solution(14435450560687561985)
XLA Ops:
  0.6 44.1 %shard_map.76 = (f32[1,64]{1,0:T(1,128)}, f32[1,104]{1,0:T(1,128)}, f32[32,64]{1,0:T(8,128)}) custom-call(f32[32,64]{1,0:T(8,128)} %src_hbm.1, f32[32,104]{1,0:T(8,128)} %tgt_hbm.1, f32[1,104]{1,0:T(1,128)} %bitcast.5, f32[1,64]{1,0:T(1,128)} %bitcast.6, f32[1,104]{1,0:T(1,128)} %bitcast.7), custom_call_target="tpu_custom_call" | custom-call | tf_op jit(solution)/shard_map/pallas_call | solution.py:365
  44.7 0.0 copy-start.1
  44.8 0.6 %copy-done.1 = f32[1,64]{1,0:T(1,128)S(1)} copy-done((f32[1,64]{1,0:T(1,128)S(1)}, f32[1,64]{1,0:T(1,128)}, u32[]{:S(2)}) %copy-start.1) | copy-done | bytes 280
  45.4 0.0 copy-start
  45.4 0.5 %copy.11 = f32[64]{0:T(128)} copy(f32[64]{0:T(128)S(1)} %bitcast.9) | data formatting | bytes 512
  45.9 0.1 copy-done
  46.0 0.5 %copy.12 = f32[104]{0:T(128)} copy(f32[104]{0:T(128)S(1)} %bitcast.8) | data formatting | bytes 832
  46.5 1.3 %copy.13 = f32[32,64]{1,0:T(8,128)} copy(f32[32,64]{1,0:T(8,128)} %get-tuple-element.14) | data formatting | bytes 16384
Async XLA Ops:
  44.7 0.6 %copy-start.1 = (f32[1,64]{1,0:T(1,128)S(1)}, f32[1,64]{1,0:T(1,128)}, u32[]{:S(2)}) copy-start(f32[1,64]{1,0:T(1,128)} %get-tuple-element.6) | copy-start | bytes 772
  45.4 0.6 %copy-start = (f32[1,104]{1,0:T(1,128)S(1)}, f32[1,104]{1,0:T(1,128)}, u32[]{:S(2)}) copy-start(f32[1,104]{1,0:T(1,128)} %get-tuple-element.7) | copy-start | bytes 1252

commit v3 on v2

--- a/solution.py
+++ b/solution.py
@@ -21,7 +21,7 @@
 DIM = 32
 SRC_LINES = 17
 TGT_LINES = 34
-HALVES = ((0, 1024), (1024, 640))
+HALVES = ((0, 640), (640, 1024))
 
 
 def ring(d, n):
@@ -32,12 +32,9 @@
     [(y, x) for y in range(4) for x in range(4) if y or x],
     key=lambda o: -(ring(o[0], 4) + ring(o[1], 4)),
 )
-SRC_PEERS = sorted(
-    [(z, c) for z in range(8) for c in range(2) if z or c],
-    key=lambda o: (-ring(o[0], 8), o[1]),
-)
 Z_PEERS = (4, 3, 5, 2, 6, 1, 7)
-Z_ARRIVALS = (1, 7, 2, 6, 3, 5, 4)
+Z_NEAR = (1, 7, 2, 6)
+Z_FAR = (3, 5, 4)
 
 
 def dot(a, b):
@@ -95,9 +92,9 @@
     f_ref, g_ref, p_ref,
     src_v, tgt_v, pot_v, slw_v, tlw_v,
     pad, smsg, tmsg, srecv, trecv,
-    xr, yr, xt, yt, tl,
-    slw, tlw, lpart, lsend, lrecv, gsend, grecv, moms, tops, msend, mrecv, lall, gall,
-    in_sem, s_send, s_recv, t_send, t_recv, l_send, l_recv, g_send, g_recv, m_send, m_recv,
+    xr, yr, xt, yt, tl, ya, held, peak, scr,
+    slw, tlw, lpart, lsend, lrecv, csend, crecv, gsend, grecv, moms, tops, msend, mrecv, lall, gall,
+    in_sem, s_send, s_recv, t_send, t_recv, l_send, l_recv, g_send, g_recv, m_send, m_recv, c_send, c_recv,
 ):
     me_t = lax.axis_index("tgt")
     me_s = lax.axis_index("src")
@@ -113,7 +110,7 @@
     barrier = pltpu.get_barrier_semaphore()
     for offset in TGT_PEERS:
         pl.semaphore_signal(barrier, inc=1, device_id={"tgt": at_t(offset)}, device_id_type=MESH)
-    for offset in SRC_PEERS:
+    for offset in [(z, 0) for z in Z_PEERS] + [(0, 1)]:
         pl.semaphore_signal(barrier, inc=1, device_id={"src": at_s(offset)}, device_id_type=MESH)
 
     inputs = [
@@ -144,7 +141,7 @@
     )
     tmsg[DIM + 1 : DIM + 2, 0:OWN_COLS] = LOG2E * tlw_v[...]
 
-    pl.semaphore_wait(barrier, 2 * (GROUP - 1))
+    pl.semaphore_wait(barrier, len(TGT_PEERS) + len(Z_PEERS) + 1)
     sent = []
 
     def to_t(offset, src, dst, send, recv):
@@ -179,50 +176,84 @@
     zeros48 = jnp.zeros((48, 128), BF16)
     zeros56 = jnp.zeros((56, 128), F32)
 
+    partner = lax.rem(me_c + 1, 2)
+
+    def cells(slot):
+        return trecv.at[slot, 0:TGT_LINES]
+
+    def forward(n, z):
+        slot = lax.rem(me_z + z, 8) * 2 + me_c
+        arrive(cells(slot), t_recv.at[slot])
+        to_s((0, 1), slot, cells(slot), cells(slot), t_send.at[8 + n], t_recv)
+
+    def operand(n, slots):
+        tops_t, tails_t = [], []
+        for slot in slots:
+            block = trecv[slot]
+            y1, y2, y3 = split3(block[0:DIM])
+            tops_t.append(jnp.transpose(jnp.concatenate([y1, y2, y1, y2], 0))[0:OWN_COLS])
+            tail = jnp.concatenate([y3, y1, bias_rows(block[DIM : DIM + 1]), zeros56], 0)
+            tails_t.append(jnp.transpose(tail)[0:OWN_COLS])
+        ya[n, :, 0:128] = jnp.concatenate(tops_t, 0).astype(BF16)
+        ya[n, :, 128:256] = jnp.concatenate(tails_t, 0).astype(BF16)
+
+    def mine(z):
+        return lax.rem(me_z + z, 8) * 2 + me_c
+
+    def other(z):
+        return lax.rem(me_z + z, 8) * 2 + partner
+
+    def first(n):
+        scores = dot(ya[n], xr[...])
+        held[n % 2] = scores
+        peak[n % 2] = jnp.max(scores, 0, keepdims=True)
+
+    def second(n):
+        top = peak[n % 2]
+        part = top + jnp.log(jnp.sum(jnp.exp2(held[n % 2] - top), 0, keepdims=True)) * LOG2E
+        for p in range(8):
+            lpart[n, p : p + 1, :] = part[:, 128 * p : 128 * p + 128]
+
+    arrive(cells(other(0)), t_recv.at[other(0)])
+    operand(0, (me_s, other(0)))
+    for n, z in enumerate(Z_NEAR):
+        forward(n, z)
+    operand(1, (mine(1), mine(7)))
+    operand(2, (mine(2), mine(6)))
+
     for offset in reversed(TGT_PEERS):
         slot = at_t(offset)
         arrive(srecv.at[slot, 0:SRC_LINES], s_recv.at[slot])
     for p in range(8):
         a, b = srecv[2 * p], srecv[2 * p + 1]
-        first = jnp.where(low, a[0:16], pltpu.roll(b[0:16], 64, 1))
-        second = jnp.where(low, pltpu.roll(a[0:16], 64, 1), b[0:16])
-        x1, x2, x3 = split3(jnp.concatenate([first, second], 0) * (2.0 * SCALE))
+        one = jnp.where(low, a[0:16], pltpu.roll(b[0:16], 64, 1))
+        two = jnp.where(low, pltpu.roll(a[0:16], 64, 1), b[0:16])
+        x1, x2, x3 = split3(jnp.concatenate([one, two], 0) * (2.0 * SCALE))
         at = slice(128 * p, 128 * p + 128)
         slw[p : p + 1, :] = jnp.where(low[0:1], a[16:17], pltpu.roll(b[16:24], 64, 1)[0:1])
         xr[0:128, at] = jnp.concatenate([x1, x1, x2, x2], 0).astype(BF16)
         xr[128:192, at] = jnp.concatenate([x1, x3], 0).astype(BF16)
         xr[192:208, at] = ones16
         xr[208:256, at] = zeros48
-
-    def take(n, z):
-        pair = lax.rem(me_z + z, 8)
-        tops_t, tails_t = [], []
-        for c in range(2):
-            block = trecv[2 * pair + c]
-            y1, y2, y3 = split3(block[0:DIM])
-            tops_t.append(jnp.transpose(jnp.concatenate([y1, y2, y1, y2], 0))[0:OWN_COLS])
-            tail = jnp.concatenate([y3, y1, bias_rows(block[DIM : DIM + 1]), zeros56], 0)
-            tails_t.append(jnp.transpose(tail)[0:OWN_COLS])
-        at = pl.ds(pl.multiple_of(pair * (2 * OWN_COLS), 16), 2 * OWN_COLS)
-        yt[at, 0:128] = jnp.concatenate(tops_t, 0).astype(BF16)
-        yt[at, 128:256] = jnp.concatenate(tails_t, 0).astype(BF16)
-        part = lse(dot(yt[at, :], xr[...]))
-        for p in range(8):
-            lpart[n, p : p + 1, :] = part[:, 128 * p : 128 * p + 128]
-
-    partner = lax.rem(me_c + 1, 2)
-    arrive(trecv.at[me_z * 2 + partner, 0:TGT_LINES], t_recv.at[me_z * 2 + partner])
-    for n in range(8):
-        if n < 7:
-            pair = lax.rem(me_z + Z_ARRIVALS[n], 8)
-            slot = pair * 2 + me_c
-            here = trecv.at[slot, 0:TGT_LINES]
-            arrive(here, t_recv.at[slot])
-            to_s((0, 1), slot, here, here, t_send.at[8 + n], t_recv)
-        take(n, 0 if n == 0 else Z_ARRIVALS[n - 1])
-        if n < 7:
-            slot = pair * 2 + partner
-            arrive(trecv.at[slot, 0:TGT_LINES], t_recv.at[slot])
+    for n, z in enumerate(Z_FAR):
+        forward(4 + n, z)
+    operand(3, (mine(3), mine(5)))
+    first(0)
+    first(1)
+    second(0)
+    first(2)
+    second(1)
+    first(3)
+    second(2)
+    late = [mine(4)] + [other(z) for z in (1, 7, 2, 6, 3, 5, 4)]
+    for n in range(4, 8):
+        slots = late[2 * n - 8 : 2 * n - 6]
+        for slot in slots[1 if n == 4 else 0 :]:
+            arrive(cells(slot), t_recv.at[slot])
+        operand(n, slots)
+        first(n)
+        second(n - 1)
+    second(7)
     lsend[...] = combine([lpart[n] for n in range(8)])
     for n, offset in enumerate(TGT_PEERS):
         to_t(offset, lsend, lrecv.at[me_t], l_send.at[n], l_recv)
@@ -247,6 +278,7 @@
         yr[128:192, at] = jnp.concatenate([y3, y1], 0).astype(BF16)
         yr[192:208, at] = ones16
         yr[208:256, at] = zeros48
+        yt[at, 0:128] = jnp.transpose(jnp.concatenate([y1, y2, y1, y2], 0)).astype(BF16)
         tl[0:32, at] = y1.astype(BF16)
         tl[32:48, at] = jnp.ones((16, 128), BF16)
         tl[48:80, at] = y2.astype(BF16)
@@ -262,46 +294,91 @@
         tail = jnp.concatenate([xr[128:192, at].astype(F32), bias_rows(bias), zeros56], 0)
         xt[at, 128:256] = jnp.transpose(tail).astype(BF16)
 
-    for half, (base, count) in enumerate(HALVES):
-        for start in range(0, count, 256):
-            width = min(256, count - start)
-            part = lse(dot(xt[...], yr[:, base + start : base + start + width]))
-            for h in range(width // 128):
-                line = start // 128 + h
-                gsend[half, line : line + 1, :] = part[:, 128 * h : 128 * h + 128]
-        lines = count // 128
-        for n, offset in enumerate(SRC_PEERS):
-            to_s(offset, half * GROUP + me_s, gsend.at[half, 0:lines], grecv.at[half, me_s, 0:lines],
-                 g_send.at[half * GROUP + n], g_recv)
-    for half in range(2):
-        grecv[half, me_s] = gsend[half]
+    jobs = [
+        (half, base, start, min(256, count - start))
+        for half, (base, count) in enumerate(HALVES)
+        for start in range(0, count, 256)
+    ]
+
+    def first(n):
+        half, base, start, width = jobs[n]
+        scores = dot(xt[...], yr[:, base + start : base + start + width])
+        scr[n % 2, :, 0:width] = scores
+        peak[n % 2, :, 0:width] = jnp.max(scores, 0, keepdims=True)
+
+    def second(n):
+        half, base, start, width = jobs[n]
+        top = peak[n % 2, :, 0:width]
+        part = top + jnp.log(
+            jnp.sum(jnp.exp2(scr[n % 2, :, 0:width] - top), 0, keepdims=True)
+        ) * LOG2E
+        for h in range(width // 128):
+            line = start // 128 + h
+            csend[half, line : line + 1, :] = part[:, 128 * h : 128 * h + 128]
+
+    lines = [count // 128 for base, count in HALVES]
+
+    def to_partner(half):
+        there = crecv.at[half, 0 : lines[half]]
+        copy = pltpu.make_async_remote_copy(
+            src_ref=csend.at[half, 0 : lines[half]], dst_ref=there,
+            send_sem=c_send.at[half], recv_sem=c_recv.at[half],
+            device_id={"src": at_s((0, 1))}, device_id_type=MESH,
+        )
+        copy.start()
+        sent.append(copy)
+
+    def to_line(half):
+        there = crecv.at[half, 0 : lines[half]]
+        arrive(there, c_recv.at[half])
+        gsend[half] = combine([csend[half], crecv[half]])
+        for n, z in enumerate(Z_PEERS):
+            to_s((z, 0), half * 8 + me_z, gsend.at[half, 0 : lines[half]],
+                 grecv.at[half, me_z, 0 : lines[half]], g_send.at[half * 8 + n], g_recv)
+        grecv[half, me_z] = gsend[half]
+
+    for n in range(len(jobs) + 1):
+        if n < len(jobs):
+            first(n)
+        if n > 0:
+            second(n - 1)
+            if n == 3:
+                to_partner(0)
+            if n == 5:
+                to_line(0)
+    to_partner(1)
+    to_line(1)
 
     row = lall[pl.ds(me_y * 2 + me_x // 2, 1), :]
     row = jnp.where(lax.rem(me_t, 2) == 1, pltpu.roll(row, 64, 1), row)
     f_ref[...] = (src_sq - (EPSILON / LOG2E) * row)[:, 0:OWN_ROWS]
 
     for half, (base, count) in enumerate(HALVES):
-        lines = count // 128
-        for offset in reversed(SRC_PEERS):
-            slot = at_s(offset)
-            arrive(grecv.at[half, slot, 0:lines], g_recv.at[half * GROUP + slot])
-        if half == 1:
-            pass
-        col_lse = combine([grecv[half, k] for k in range(GROUP)])
-        gall[8 * half : 8 * half + 8, :] = col_lse
-        for line in range(lines):
+        for z in reversed(Z_PEERS):
+            slot = lax.rem(me_z + z, 8)
+            arrive(grecv.at[half, slot, 0 : lines[half]], g_recv.at[half * 8 + slot])
+        col_lse = combine([grecv[half, k] for k in range(8)])
+        gall[base // 128 : base // 128 + lines[half], :] = col_lse[0 : lines[half]]
+        for line in range(lines[half]):
             at = slice(base + 128 * line, base + 128 * line + 128)
             q = base // 128 + line
             bias = tlw[q : q + 1, :] - col_lse[line : line + 1, :]
             tail = jnp.concatenate([yr[128:192, at].astype(F32), bias_rows(bias), zeros56], 0)
             yt[at, 128:256] = jnp.transpose(tail).astype(BF16)
         span = slice(base, base + count)
-        for order in ((0, 1, 2, 3), (2, 1, 3, 0))[half]:
+        orders = (2, 1, 3, 0)
+
+        def first(n):
+            columns = pl.ds(pl.multiple_of(lax.rem(me_y + orders[n], 4) * 256, 256), 256)
+            scores = dot(yt[span, :], xr[:, columns])
+            scr[n % 2, 0:count, :] = scores
+            peak[n % 2, :, 0:256] = jnp.max(scores, 0, keepdims=True)
+
+        def second(n):
+            order = orders[n]
             tile = lax.rem(me_y + order, 4)
-            columns = pl.ds(pl.multiple_of(tile * 256, 256), 256)
-            scores = dot(yt[span, :], xr[:, columns])
-            top = jnp.max(scores, 0, keepdims=True)
-            weights = jnp.exp2(scores - top)
+            top = peak[n % 2, :, 0:256]
+            weights = jnp.exp2(scr[n % 2, 0:count, :] - top)
             high = weights.astype(BF16)
             rest = (weights - high.astype(F32)).astype(BF16)
             main = dot(tl[0:80, span], high)
@@ -309,13 +386,13 @@
                 [main[0:32] + main[48:80], main[32:40]], 0
             ) + dot(tl[0:48, span], rest)[0:40]
             if half == 0:
-                moms[order] = moments
-                tops[order] = jnp.broadcast_to(top, (8, 256))
-                continue
-            before = tops[order]
+                moms[n] = moments
+                tops[n] = jnp.broadcast_to(top, (8, 256))
+                return
+            before = tops[n]
             both = jnp.maximum(before, top)
             fix_a, fix_b = jnp.exp2(before - both), jnp.exp2(top - both)
-            moments = moms[order] * fix_a[0:1] + moments * fix_b[0:1]
+            moments = moms[n] * fix_a[0:1] + moments * fix_b[0:1]
             for u in range(4):
                 lanes = slice(128 * (u // 2), 128 * (u // 2) + 128)
                 one, two = moments[0:16, lanes], moments[16:32, lanes]
@@ -330,6 +407,12 @@
                 slot = tile * 4 + lax.rem(me_x + x, 4)
                 to_t((order, x), msend.at[slot, 0:SRC_LINES], mrecv.at[me_t, 0:SRC_LINES],
                      m_send.at[order * 4 + x], m_recv)
+
+        for n in range(5):
+            if n < 4:
+                first(n)
+            if n > 0:
+                second(n - 1)
     mrecv[me_t] = msend[me_t]
 
     start = me_s * OWN_COLS
@@ -387,13 +470,19 @@
             pltpu.VMEM((ROWS, 256), BF16),
             pltpu.VMEM((COLS, 256), BF16),
             pltpu.VMEM((80, COLS), BF16),
+            pltpu.VMEM((8, 2 * OWN_COLS, 256), BF16),
+            pltpu.VMEM((2, 2 * OWN_COLS, ROWS), F32),
+            pltpu.VMEM((2, 1, ROWS), F32),
+            pltpu.VMEM((2, ROWS, 256), F32),
             pltpu.VMEM((8, 128), F32),
             pltpu.VMEM((16, 128), F32),
             pltpu.VMEM((8, 8, 128), F32),
             pltpu.VMEM((8, 128), F32),
             pltpu.VMEM((GROUP, 8, 128), F32),
             pltpu.VMEM((2, 8, 128), F32),
-            pltpu.VMEM((2, GROUP, 8, 128), F32),
+            pltpu.VMEM((2, 8, 128), F32),
+            pltpu.VMEM((2, 8, 128), F32),
+            pltpu.VMEM((2, 8, 8, 128), F32),
             pltpu.VMEM((4, 40, 256), F32),
             pltpu.VMEM((4, 8, 256), F32),
             pltpu.VMEM((GROUP, 24, 128), F32),
@@ -403,8 +492,8 @@
             pltpu.SemaphoreType.DMA((5,)),
         ]
         + [pltpu.SemaphoreType.DMA((GROUP,))] * 6
-        + [pltpu.SemaphoreType.DMA((2 * GROUP,))] * 2
-        + [pltpu.SemaphoreType.DMA((GROUP,))] * 2,
+        + [pltpu.SemaphoreType.DMA((GROUP,))] * 4
+        + [pltpu.SemaphoreType.DMA((2,))] * 2,
         compiler_params=pltpu.CompilerParams(
             collective_id=0, has_side_effects=True, vmem_limit_bytes=60 * 1024 * 1024
         ),

time: 48.1 us -> 43.1 us (0.90)
  Pallas kernels: 44.1 us -> 39.1 us
    pallas_call x1, Pallas kernels: 44.1 us -> 39.1 us  [body(): pl.pallas_call(kernel, out_shape=(jax.ShapeDtypeStruct((1, OWN_ROWS), F32...]
where the time goes in v3:
time: 43.1 us; the launch traced here: 42.8 us
  Pallas kernels  39.1 us (91%)
  local copies, waits for them, and re-layouts  3.07 us (7%)
  between operations  0.65 us (2%)
    pallas_call x1, Pallas kernels, body(): pl.pallas_call(kernel, out_shape=(jax.ShapeDtypeStruct((1, OWN_ROWS), F32...  39.1 us
    unnamed x7, local copies, waits for them, and re-layouts  3.07 us

profile of v3, /device:TPU:1, one launch (start us, length us, event | category | flops | bytes accessed | tf_op | source)
XLA Modules:
  0.0 42.8 jit_solution(2040572048363552354)
XLA Ops:
  0.6 39.1 %shard_map.76 = (f32[1,64]{1,0:T(1,128)}, f32[1,104]{1,0:T(1,128)}, f32[32,64]{1,0:T(8,128)}) custom-call(f32[32,64]{1,0:T(8,128)} %src_hbm.1, f32[32,104]{1,0:T(8,128)} %tgt_hbm.1, f32[1,104]{1,0:T(1,128)} %bitcast.5, f32[1,64]{1,0:T(1,128)} %bitcast.6, f32[1,104]{1,0:T(1,128)} %bitcast.7), custom_call_target="tpu_custom_call" | custom-call | tf_op jit(solution)/shard_map/pallas_call | solution.py:448
  39.7 0.0 copy-start.1
  39.7 0.6 %copy-done.1 = f32[1,64]{1,0:T(1,128)S(1)} copy-done((f32[1,64]{1,0:T(1,128)S(1)}, f32[1,64]{1,0:T(1,128)}, u32[]{:S(2)}) %copy-start.1) | copy-done | bytes 280
  40.3 0.0 copy-start
  40.3 0.5 %copy.11 = f32[64]{0:T(128)} copy(f32[64]{0:T(128)S(1)} %bitcast.9) | data formatting | bytes 512
  40.9 0.1 copy-done
  41.0 0.5 %copy.12 = f32[104]{0:T(128)} copy(f32[104]{0:T(128)S(1)} %bitcast.8) | data formatting | bytes 832
  41.5 1.3 %copy.13 = f32[32,64]{1,0:T(8,128)} copy(f32[32,64]{1,0:T(8,128)} %get-tuple-element.14) | data formatting | bytes 16384
Async XLA Ops:
  39.7 0.6 %copy-start.1 = (f32[1,64]{1,0:T(1,128)S(1)}, f32[1,64]{1,0:T(1,128)}, u32[]{:S(2)}) copy-start(f32[1,64]{1,0:T(1,128)} %get-tuple-element.6) | copy-start | bytes 772
  40.3 0.6 %copy-start = (f32[1,104]{1,0:T(1,128)S(1)}, f32[1,104]{1,0:T(1,128)}, u32[]{:S(2)}) copy-start(f32[1,104]{1,0:T(1,128)} %get-tuple-element.7) | copy-start | bytes 1252

commit v4 on v3

--- a/solution.py
+++ b/solution.py
@@ -21,7 +21,6 @@
 DIM = 32
 SRC_LINES = 17
 TGT_LINES = 34
-HALVES = ((0, 640), (640, 1024))
 
 
 def ring(d, n):
@@ -93,7 +92,7 @@
     src_v, tgt_v, pot_v, slw_v, tlw_v,
     pad, smsg, tmsg, srecv, trecv,
     xr, yr, xt, yt, tl, ya, held, peak, scr,
-    slw, tlw, lpart, lsend, lrecv, csend, crecv, gsend, grecv, moms, tops, msend, mrecv, lall, gall,
+    slw, tlw, lpart, lsend, lrecv, csend, crecv, gsend, grecv, msend, mrecv, lall, gall,
     in_sem, s_send, s_recv, t_send, t_recv, l_send, l_recv, g_send, g_recv, m_send, m_recv, c_send, c_recv,
 ):
     me_t = lax.axis_index("tgt")
@@ -294,125 +293,90 @@
         tail = jnp.concatenate([xr[128:192, at].astype(F32), bias_rows(bias), zeros56], 0)
         xt[at, 128:256] = jnp.transpose(tail).astype(BF16)
 
-    jobs = [
-        (half, base, start, min(256, count - start))
-        for half, (base, count) in enumerate(HALVES)
-        for start in range(0, count, 256)
-    ]
-
     def first(n):
-        half, base, start, width = jobs[n]
-        scores = dot(xt[...], yr[:, base + start : base + start + width])
-        scr[n % 2, :, 0:width] = scores
+        width = min(256, COLS - 256 * n)
+        scores = dot(xt[...], yr[:, 256 * n : 256 * n + width])
+        scr[n % 2, 0:ROWS, 0:width] = scores
         peak[n % 2, :, 0:width] = jnp.max(scores, 0, keepdims=True)
 
     def second(n):
-        half, base, start, width = jobs[n]
+        width = min(256, COLS - 256 * n)
         top = peak[n % 2, :, 0:width]
         part = top + jnp.log(
-            jnp.sum(jnp.exp2(scr[n % 2, :, 0:width] - top), 0, keepdims=True)
+            jnp.sum(jnp.exp2(scr[n % 2, 0:ROWS, 0:width] - top), 0, keepdims=True)
         ) * LOG2E
         for h in range(width // 128):
-            line = start // 128 + h
-            csend[half, line : line + 1, :] = part[:, 128 * h : 128 * h + 128]
-
-    lines = [count // 128 for base, count in HALVES]
-
-    def to_partner(half):
-        there = crecv.at[half, 0 : lines[half]]
-        copy = pltpu.make_async_remote_copy(
-            src_ref=csend.at[half, 0 : lines[half]], dst_ref=there,
-            send_sem=c_send.at[half], recv_sem=c_recv.at[half],
-            device_id={"src": at_s((0, 1))}, device_id_type=MESH,
-        )
-        copy.start()
-        sent.append(copy)
-
-    def to_line(half):
-        there = crecv.at[half, 0 : lines[half]]
-        arrive(there, c_recv.at[half])
-        gsend[half] = combine([csend[half], crecv[half]])
-        for n, z in enumerate(Z_PEERS):
-            to_s((z, 0), half * 8 + me_z, gsend.at[half, 0 : lines[half]],
-                 grecv.at[half, me_z, 0 : lines[half]], g_send.at[half * 8 + n], g_recv)
-        grecv[half, me_z] = gsend[half]
-
-    for n in range(len(jobs) + 1):
-        if n < len(jobs):
+            csend[2 * n + h : 2 * n + h + 1, :] = part[:, 128 * h : 128 * h + 128]
+
+    for n in range(8):
+        if n < 7:
             first(n)
         if n > 0:
             second(n - 1)
-            if n == 3:
-                to_partner(0)
-            if n == 5:
-                to_line(0)
-    to_partner(1)
-    to_line(1)
+    there = crecv.at[0:13]
+    copy = pltpu.make_async_remote_copy(
+        src_ref=csend.at[0:13], dst_ref=there, send_sem=c_send.at[0], recv_sem=c_recv.at[0],
+        device_id={"src": at_s((0, 1))}, device_id_type=MESH,
+    )
+    copy.start()
+    sent.append(copy)
+    arrive(there, c_recv.at[0])
+    gsend[...] = combine([csend[...], crecv[...]])
+    for n, z in enumerate(Z_PEERS):
+        to_s((z, 0), me_z, gsend.at[0:13], grecv.at[me_z, 0:13], g_send.at[n], g_recv)
+    grecv[me_z] = gsend[...]
 
     row = lall[pl.ds(me_y * 2 + me_x // 2, 1), :]
     row = jnp.where(lax.rem(me_t, 2) == 1, pltpu.roll(row, 64, 1), row)
     f_ref[...] = (src_sq - (EPSILON / LOG2E) * row)[:, 0:OWN_ROWS]
 
-    for half, (base, count) in enumerate(HALVES):
-        for z in reversed(Z_PEERS):
-            slot = lax.rem(me_z + z, 8)
-            arrive(grecv.at[half, slot, 0 : lines[half]], g_recv.at[half * 8 + slot])
-        col_lse = combine([grecv[half, k] for k in range(8)])
-        gall[base // 128 : base // 128 + lines[half], :] = col_lse[0 : lines[half]]
-        for line in range(lines[half]):
-            at = slice(base + 128 * line, base + 128 * line + 128)
-            q = base // 128 + line
-            bias = tlw[q : q + 1, :] - col_lse[line : line + 1, :]
-            tail = jnp.concatenate([yr[128:192, at].astype(F32), bias_rows(bias), zeros56], 0)
-            yt[at, 128:256] = jnp.transpose(tail).astype(BF16)
-        span = slice(base, base + count)
-        orders = (2, 1, 3, 0)
-
-        def first(n):
-            columns = pl.ds(pl.multiple_of(lax.rem(me_y + orders[n], 4) * 256, 256), 256)
-            scores = dot(yt[span, :], xr[:, columns])
-            scr[n % 2, 0:count, :] = scores
-            peak[n % 2, :, 0:256] = jnp.max(scores, 0, keepdims=True)
-
-        def second(n):
-            order = orders[n]
-            tile = lax.rem(me_y + order, 4)
-            top = peak[n % 2, :, 0:256]
-            weights = jnp.exp2(scr[n % 2, 0:count, :] - top)
-            high = weights.astype(BF16)
-            rest = (weights - high.astype(F32)).astype(BF16)
-            main = dot(tl[0:80, span], high)
-            moments = jnp.concatenate(
-                [main[0:32] + main[48:80], main[32:40]], 0
-            ) + dot(tl[0:48, span], rest)[0:40]
-            if half == 0:
-                moms[n] = moments
-                tops[n] = jnp.broadcast_to(top, (8, 256))
-                return
-            before = tops[n]
-            both = jnp.maximum(before, top)
-            fix_a, fix_b = jnp.exp2(before - both), jnp.exp2(top - both)
-            moments = moms[n] * fix_a[0:1] + moments * fix_b[0:1]
-            for u in range(4):
-                lanes = slice(128 * (u // 2), 128 * (u // 2) + 128)
-                one, two = moments[0:16, lanes], moments[16:32, lanes]
-                three, four = moments[32:40, lanes], both[:, lanes]
-                if u % 2 == 0:
-                    two, four = pltpu.roll(two, 64, 1), pltpu.roll(four, 64, 1)
-                else:
-                    one, three = pltpu.roll(one, 64, 1), pltpu.roll(three, 64, 1)
-                msend[tile * 4 + u, 0:16, :] = jnp.where(low, one, two)
-                msend[tile * 4 + u, 16:24, :] = jnp.where(low[0:8], three, four)
-            for x in range(0 if order else 1, 4):
-                slot = tile * 4 + lax.rem(me_x + x, 4)
-                to_t((order, x), msend.at[slot, 0:SRC_LINES], mrecv.at[me_t, 0:SRC_LINES],
-                     m_send.at[order * 4 + x], m_recv)
-
-        for n in range(5):
-            if n < 4:
-                first(n)
-            if n > 0:
-                second(n - 1)
+    for z in reversed(Z_PEERS):
+        slot = lax.rem(me_z + z, 8)
+        arrive(grecv.at[slot, 0:13], g_recv.at[slot])
+    col_lse = combine([grecv[k] for k in range(8)])
+    gall[...] = col_lse
+    for q in range(13):
+        at = slice(128 * q, 128 * q + 128)
+        bias = tlw[q : q + 1, :] - col_lse[q : q + 1, :]
+        tail = jnp.concatenate([yr[128:192, at].astype(F32), bias_rows(bias), zeros56], 0)
+        yt[at, 128:256] = jnp.transpose(tail).astype(BF16)
+    orders = (2, 1, 3, 0)
+
+    def first(n):
+        columns = pl.ds(pl.multiple_of(lax.rem(me_y + orders[n], 4) * 256, 256), 256)
+        scores = dot(yt[...], xr[:, columns])
+        scr[n % 2] = scores
+        peak[n % 2, :, 0:256] = jnp.max(scores, 0, keepdims=True)
+
+    def second(n):
+        order = orders[n]
+        tile = lax.rem(me_y + order, 4)
+        top = peak[n % 2, :, 0:256]
+        weights = jnp.exp2(scr[n % 2] - top)
+        high = weights.astype(BF16)
+        rest = (weights - high.astype(F32)).astype(BF16)
+        main = dot(tl[...], high)
+        moments = jnp.concatenate([main[0:32] + main[48:80], main[32:40]], 0) + dot(tl[0:48, :], rest)[0:40]
+        for u in range(4):
+            lanes = slice(128 * (u // 2), 128 * (u // 2) + 128)
+            one, two = moments[0:16, lanes], moments[16:32, lanes]
+            three, four = moments[32:40, lanes], jnp.broadcast_to(top[:, lanes], (8, 128))
+            if u % 2 == 0:
+                two, four = pltpu.roll(two, 64, 1), pltpu.roll(four, 64, 1)
+            else:
+                one, three = pltpu.roll(one, 64, 1), pltpu.roll(three, 64, 1)
+            msend[tile * 4 + u, 0:16, :] = jnp.where(low, one, two)
+            msend[tile * 4 + u, 16:24, :] = jnp.where(low[0:8], three, four)
+        for x in range(0 if order else 1, 4):
+            slot = tile * 4 + lax.rem(me_x + x, 4)
+            to_t((order, x), msend.at[slot, 0:SRC_LINES], mrecv.at[me_t, 0:SRC_LINES],
+                 m_send.at[order * 4 + x], m_recv)
+
+    for n in range(5):
+        if n < 4:
+            first(n)
+        if n > 0:
+            second(n - 1)
     mrecv[me_t] = msend[me_t]
 
     start = me_s * OWN_COLS
@@ -473,18 +437,16 @@
             pltpu.VMEM((8, 2 * OWN_COLS, 256), BF16),
             pltpu.VMEM((2, 2 * OWN_COLS, ROWS), F32),
             pltpu.VMEM((2, 1, ROWS), F32),
-            pltpu.VMEM((2, ROWS, 256), F32),
+            pltpu.VMEM((2, COLS, 256), F32),
             pltpu.VMEM((8, 128), F32),
             pltpu.VMEM((16, 128), F32),
             pltpu.VMEM((8, 8, 128), F32),
             pltpu.VMEM((8, 128), F32),
             pltpu.VMEM((GROUP, 8, 128), F32),
-            pltpu.VMEM((2, 8, 128), F32),
-            pltpu.VMEM((2, 8, 128), F32),
-            pltpu.VMEM((2, 8, 128), F32),
-            pltpu.VMEM((2, 8, 8, 128), F32),
-            pltpu.VMEM((4, 40, 256), F32),
-            pltpu.VMEM((4, 8, 256), F32),
+            pltpu.VMEM((16, 128), F32),
+            pltpu.VMEM((16, 128), F32),
+            pltpu.VMEM((16, 128), F32),
+            pltpu.VMEM((8, 16, 128), F32),
             pltpu.VMEM((GROUP, 24, 128), F32),
             pltpu.VMEM((GROUP, 24, 128), F32),
             pltpu.VMEM((8, 128), F32),
@@ -493,7 +455,7 @@
         ]
         + [pltpu.SemaphoreType.DMA((GROUP,))] * 6
         + [pltpu.SemaphoreType.DMA((GROUP,))] * 4
-        + [pltpu.SemaphoreType.DMA((2,))] * 2,
+        + [pltpu.SemaphoreType.DMA((1,))] * 2,
         compiler_params=pltpu.CompilerParams(
             collective_id=0, has_side_effects=True, vmem_limit_bytes=60 * 1024 * 1024
         ),

time: 43.1 us -> 43.2 us (level)
  no operation moved by 1% of the time
where the time goes in v4:
time: 43.2 us; the launch traced here: 42.9 us
  Pallas kernels  39.2 us (91%)
  local copies, waits for them, and re-layouts  3.07 us (7%)
  between operations  0.65 us (2%)
    pallas_call x1, Pallas kernels, body(): pl.pallas_call(kernel, out_shape=(jax.ShapeDtypeStruct((1, OWN_ROWS), F32...  39.2 us
    unnamed x7, local copies, waits for them, and re-layouts  3.07 us

profile of v4, /device:TPU:1, one launch (start us, length us, event | category | flops | bytes accessed | tf_op | source)
XLA Modules:
  0.0 42.9 jit_solution(5003712572337735432)
XLA Ops:
  0.6 39.2 %shard_map.76 = (f32[1,64]{1,0:T(1,128)}, f32[1,104]{1,0:T(1,128)}, f32[32,64]{1,0:T(8,128)}) custom-call(f32[32,64]{1,0:T(8,128)} %src_hbm.1, f32[32,104]{1,0:T(8,128)} %tgt_hbm.1, f32[1,104]{1,0:T(1,128)} %bitcast.5, f32[1,64]{1,0:T(1,128)} %bitcast.6, f32[1,104]{1,0:T(1,128)} %bitcast.7), custom_call_target="tpu_custom_call" | custom-call | tf_op jit(solution)/shard_map/pallas_call | solution.py:412
  39.8 0.0 copy-start.1
  39.8 0.6 %copy-done.1 = f32[1,64]{1,0:T(1,128)S(1)} copy-done((f32[1,64]{1,0:T(1,128)S(1)}, f32[1,64]{1,0:T(1,128)}, u32[]{:S(2)}) %copy-start.1) | copy-done | bytes 280
  40.5 0.0 copy-start
  40.5 0.5 %copy.11 = f32[64]{0:T(128)} copy(f32[64]{0:T(128)S(1)} %bitcast.9) | data formatting | bytes 512
  41.0 0.1 copy-done
  41.1 0.5 %copy.12 = f32[104]{0:T(128)} copy(f32[104]{0:T(128)S(1)} %bitcast.8) | data formatting | bytes 832
  41.6 1.3 %copy.13 = f32[32,64]{1,0:T(8,128)} copy(f32[32,64]{1,0:T(8,128)} %get-tuple-element.14) | data formatting | bytes 16384
Async XLA Ops:
  39.8 0.6 %copy-start.1 = (f32[1,64]{1,0:T(1,128)S(1)}, f32[1,64]{1,0:T(1,128)}, u32[]{:S(2)}) copy-start(f32[1,64]{1,0:T(1,128)} %get-tuple-element.6) | copy-start | bytes 772
  40.5 0.6 %copy-start = (f32[1,104]{1,0:T(1,128)S(1)}, f32[1,104]{1,0:T(1,128)}, u32[]{:S(2)}) copy-start(f32[1,104]{1,0:T(1,128)} %get-tuple-element.7) | copy-start | bytes 1252

commit v5 on v4

--- a/solution.py
+++ b/solution.py
@@ -10,6 +10,7 @@
 EPSILON = 0.05
 LOG2E = 1.0 / math.log(2.0)
 SCALE = LOG2E / EPSILON
+TOP_LOGW = -9.0 * LOG2E
 F32 = jnp.float32
 BF16 = jnp.bfloat16
 MESH = pl.DeviceIdType.MESH
@@ -32,8 +33,6 @@
     key=lambda o: -(ring(o[0], 4) + ring(o[1], 4)),
 )
 Z_PEERS = (4, 3, 5, 2, 6, 1, 7)
-Z_NEAR = (1, 7, 2, 6)
-Z_FAR = (3, 5, 4)
 
 
 def dot(a, b):
@@ -55,10 +54,11 @@
     return lax.broadcasted_iota(jnp.int32, (rows, 128), 0)
 
 
-def bias_rows(bias):
+def bias_rows(bias, at=0, other=0.0):
     one, two, three = split3(bias)
     sub = sub_iota(8)
-    return jnp.where(sub == 0, one, jnp.where(sub == 1, two, jnp.where(sub == 2, three, 0.0)))
+    rest = jnp.where(sub < 6, other, 0.0)
+    return jnp.where(sub == at, one, jnp.where(sub == at + 1, two, jnp.where(sub == at + 2, three, rest)))
 
 
 def combine(parts):
@@ -88,7 +88,7 @@
 
 def kernel(
     src_hbm, tgt_hbm, pot_hbm, slw_hbm, tlw_hbm,
-    f_ref, g_ref, p_ref,
+    out_ref,
     src_v, tgt_v, pot_v, slw_v, tlw_v,
     pad, smsg, tmsg, srecv, trecv,
     xr, yr, xt, yt, tl, ya, held, peak, scr,
@@ -164,31 +164,20 @@
 
     tgt_own = tmsg.at[0:TGT_LINES]
     for n, z in enumerate(Z_PEERS):
-        to_s((z, 0), me_s, tgt_own, trecv.at[me_s, 0:TGT_LINES], t_send.at[n], t_recv)
-    to_s((0, 1), me_s, tgt_own, trecv.at[me_s, 0:TGT_LINES], t_send.at[7], t_recv)
+        to_s((z, 0), 8 - z, tgt_own, trecv.at[0, 8 - z, 0:TGT_LINES], t_send.at[n], t_recv)
     src_own = smsg.at[0:SRC_LINES]
     for n, offset in enumerate(TGT_PEERS):
         to_t(offset, src_own, srecv.at[me_t, 0:SRC_LINES], s_send.at[n], s_recv)
     srecv[me_t] = smsg[...]
-    trecv[me_s] = tmsg[...]
+    trecv[0, 0] = tmsg[...]
     ones16 = jnp.where(sub_iota(16) < 3, 1.0, 0.0).astype(BF16)
     zeros48 = jnp.zeros((48, 128), BF16)
     zeros56 = jnp.zeros((56, 128), F32)
 
-    partner = lax.rem(me_c + 1, 2)
-
-    def cells(slot):
-        return trecv.at[slot, 0:TGT_LINES]
-
-    def forward(n, z):
-        slot = lax.rem(me_z + z, 8) * 2 + me_c
-        arrive(cells(slot), t_recv.at[slot])
-        to_s((0, 1), slot, cells(slot), cells(slot), t_send.at[8 + n], t_recv)
-
-    def operand(n, slots):
+    def operand(n):
         tops_t, tails_t = [], []
-        for slot in slots:
-            block = trecv[slot]
+        for z in (2 * n, 2 * n + 1):
+            block = trecv[z // 8, z % 8]
             y1, y2, y3 = split3(block[0:DIM])
             tops_t.append(jnp.transpose(jnp.concatenate([y1, y2, y1, y2], 0))[0:OWN_COLS])
             tail = jnp.concatenate([y3, y1, bias_rows(block[DIM : DIM + 1]), zeros56], 0)
@@ -196,12 +185,6 @@
         ya[n, :, 0:128] = jnp.concatenate(tops_t, 0).astype(BF16)
         ya[n, :, 128:256] = jnp.concatenate(tails_t, 0).astype(BF16)
 
-    def mine(z):
-        return lax.rem(me_z + z, 8) * 2 + me_c
-
-    def other(z):
-        return lax.rem(me_z + z, 8) * 2 + partner
-
     def first(n):
         scores = dot(ya[n], xr[...])
         held[n % 2] = scores
@@ -213,12 +196,10 @@
         for p in range(8):
             lpart[n, p : p + 1, :] = part[:, 128 * p : 128 * p + 128]
 
-    arrive(cells(other(0)), t_recv.at[other(0)])
-    operand(0, (me_s, other(0)))
-    for n, z in enumerate(Z_NEAR):
-        forward(n, z)
-    operand(1, (mine(1), mine(7)))
-    operand(2, (mine(2), mine(6)))
+    for z in reversed(Z_PEERS):
+        arrive(trecv.at[0, 8 - z, 0:TGT_LINES], t_recv.at[8 - z])
+    to_s((0, 1), 8, trecv.at[0, :, 0:TGT_LINES], trecv.at[1, :, 0:TGT_LINES], t_send.at[7], t_recv)
+    operand(0)
 
     for offset in reversed(TGT_PEERS):
         slot = at_t(offset)
@@ -234,22 +215,14 @@
         xr[128:192, at] = jnp.concatenate([x1, x3], 0).astype(BF16)
         xr[192:208, at] = ones16
         xr[208:256, at] = zeros48
-    for n, z in enumerate(Z_FAR):
-        forward(4 + n, z)
-    operand(3, (mine(3), mine(5)))
     first(0)
-    first(1)
-    second(0)
-    first(2)
-    second(1)
-    first(3)
-    second(2)
-    late = [mine(4)] + [other(z) for z in (1, 7, 2, 6, 3, 5, 4)]
+    for n in range(1, 4):
+        operand(n)
+        first(n)
+        second(n - 1)
+    arrive(trecv.at[1, :, 0:TGT_LINES], t_recv.at[8])
     for n in range(4, 8):
-        slots = late[2 * n - 8 : 2 * n - 6]
-        for slot in slots[1 if n == 4 else 0 :]:
-            arrive(cells(slot), t_recv.at[slot])
-        operand(n, slots)
+        operand(n)
         first(n)
         second(n - 1)
     second(7)
@@ -266,7 +239,7 @@
         lane = lane_iota(40)
         block = None
         for shard, offset, start, stop in column_pieces(q):
-            piece = trecv[shard]
+            piece = trecv[lax.rem(shard + me_c, 2), lax.rem(shard // 2 + 8 - me_z, 8)]
             shift = (start - offset) % 128
             if shift:
                 piece = pltpu.roll(piece, shift, 1)
@@ -292,6 +265,8 @@
         bias = slw[p : p + 1, :] - row_lse[p : p + 1, :]
         tail = jnp.concatenate([xr[128:192, at].astype(F32), bias_rows(bias), zeros56], 0)
         xt[at, 128:256] = jnp.transpose(tail).astype(BF16)
+        both = jnp.concatenate([bias_rows(bias, 3, 1.0), jnp.zeros((8, 128), F32)], 0)
+        xr[192:208, at] = both.astype(BF16)
 
     def first(n):
         width = min(256, COLS - 256 * n)
@@ -328,7 +303,7 @@
 
     row = lall[pl.ds(me_y * 2 + me_x // 2, 1), :]
     row = jnp.where(lax.rem(me_t, 2) == 1, pltpu.roll(row, 64, 1), row)
-    f_ref[...] = (src_sq - (EPSILON / LOG2E) * row)[:, 0:OWN_ROWS]
+    out_ref[32:33, :] = src_sq - (EPSILON / LOG2E) * row
 
     for z in reversed(Z_PEERS):
         slot = lax.rem(me_z + z, 8)
@@ -337,46 +312,35 @@
     gall[...] = col_lse
     for q in range(13):
         at = slice(128 * q, 128 * q + 128)
-        bias = tlw[q : q + 1, :] - col_lse[q : q + 1, :]
-        tail = jnp.concatenate([yr[128:192, at].astype(F32), bias_rows(bias), zeros56], 0)
+        bias = tlw[q : q + 1, :] - col_lse[q : q + 1, :] - TOP_LOGW
+        tail = jnp.concatenate([yr[128:192, at].astype(F32), bias_rows(bias, 0, 1.0), zeros56], 0)
         yt[at, 128:256] = jnp.transpose(tail).astype(BF16)
-    orders = (2, 1, 3, 0)
-
-    def first(n):
-        columns = pl.ds(pl.multiple_of(lax.rem(me_y + orders[n], 4) * 256, 256), 256)
-        scores = dot(yt[...], xr[:, columns])
-        scr[n % 2] = scores
-        peak[n % 2, :, 0:256] = jnp.max(scores, 0, keepdims=True)
-
-    def second(n):
-        order = orders[n]
+    spans = ((0, 512), (512, 1024), (1024, 1664))
+    for order in (2, 1, 3, 0):
         tile = lax.rem(me_y + order, 4)
-        top = peak[n % 2, :, 0:256]
-        weights = jnp.exp2(scr[n % 2] - top)
-        high = weights.astype(BF16)
-        rest = (weights - high.astype(F32)).astype(BF16)
-        main = dot(tl[...], high)
-        moments = jnp.concatenate([main[0:32] + main[48:80], main[32:40]], 0) + dot(tl[0:48, :], rest)[0:40]
+        columns = pl.ds(pl.multiple_of(tile * 256, 256), 256)
+        moments = None
+        for base, stop in spans:
+            weights = jnp.exp2(dot(yt[base:stop, :], xr[:, columns]))
+            high = weights.astype(BF16)
+            rest = (weights - high.astype(F32)).astype(BF16)
+            main = dot(tl[:, base:stop], high)
+            part = jnp.concatenate([main[0:32] + main[48:80], main[32:40]], 0)
+            part = part + dot(tl[0:48, base:stop], rest)[0:40]
+            moments = part if moments is None else moments + part
         for u in range(4):
             lanes = slice(128 * (u // 2), 128 * (u // 2) + 128)
-            one, two = moments[0:16, lanes], moments[16:32, lanes]
-            three, four = moments[32:40, lanes], jnp.broadcast_to(top[:, lanes], (8, 128))
+            one, two, three = moments[0:16, lanes], moments[16:32, lanes], moments[32:40, lanes]
             if u % 2 == 0:
-                two, four = pltpu.roll(two, 64, 1), pltpu.roll(four, 64, 1)
+                two = pltpu.roll(two, 64, 1)
             else:
                 one, three = pltpu.roll(one, 64, 1), pltpu.roll(three, 64, 1)
             msend[tile * 4 + u, 0:16, :] = jnp.where(low, one, two)
-            msend[tile * 4 + u, 16:24, :] = jnp.where(low[0:8], three, four)
+            msend[tile * 4 + u, 16:24, :] = three
         for x in range(0 if order else 1, 4):
             slot = tile * 4 + lax.rem(me_x + x, 4)
             to_t((order, x), msend.at[slot, 0:SRC_LINES], mrecv.at[me_t, 0:SRC_LINES],
                  m_send.at[order * 4 + x], m_recv)
-
-    for n in range(5):
-        if n < 4:
-            first(n)
-        if n > 0:
-            second(n - 1)
     mrecv[me_t] = msend[me_t]
 
     start = me_s * OWN_COLS
@@ -384,40 +348,36 @@
     here = pltpu.roll(gall[pl.ds(line, 1), :], 128 - offset, 1)
     after = pltpu.roll(gall[pl.ds(line + 1, 1), :], 128 - offset, 1)
     col = jnp.where(lane_iota(1) < 128 - offset, here, after)
-    g_ref[...] = (tgt_sq - (EPSILON / LOG2E) * col)[:, 0:OWN_COLS]
+    out_ref[33:34, :] = tgt_sq - (EPSILON / LOG2E) * col
+    out_ref[34:40, :] = jnp.zeros((6, 128), F32)
 
     for offset in reversed(TGT_PEERS):
         slot = at_t(offset)
         arrive(mrecv.at[slot, 0:SRC_LINES], m_recv.at[slot])
-    top = mrecv[0, 16:17, :]
+    acc, norm = mrecv[0, 0:16, :], mrecv[0, 16:17, :]
     for k in range(1, GROUP):
-        top = jnp.maximum(top, mrecv[k, 16:17, :])
-    acc, norm = jnp.zeros((16, 128), F32), jnp.zeros((1, 128), F32)
-    low1 = low[0:1]
-    for k in range(GROUP):
-        last = mrecv[k, 16:17, :]
-        fix = jnp.exp2(last - top)
-        fix = jnp.where(low1, pltpu.roll(fix, 64, 1), fix)
-        acc = acc + mrecv[k, 0:16, :] * fix
-        norm = norm + last * fix
-    ratio = acc / jnp.where(low1, norm, pltpu.roll(norm, 64, 1))
-    p_ref[0:16, :] = ratio[:, 0:OWN_ROWS]
-    p_ref[16:32, :] = pltpu.roll(ratio, 64, 1)[:, 0:OWN_ROWS]
+        acc = acc + mrecv[k, 0:16, :]
+        norm = norm + mrecv[k, 16:17, :]
+    ratio = acc / jnp.where(low[0:1], norm, pltpu.roll(norm, 64, 1))
+    out_ref[0:16, :] = ratio
+    out_ref[16:32, :] = pltpu.roll(ratio, 64, 1)
     for copy in sent:
         copy.wait_send()
 
 
+def deliver(out_ref, f_ref, g_ref, p_ref):
+    f_ref[...] = out_ref[32:33, 0:OWN_ROWS]
+    g_ref[...] = out_ref[33:34, 0:OWN_COLS]
+    p_ref[...] = out_ref[0:DIM, 0:OWN_ROWS]
+
+
 def body(source, target, target_pot, source_logw, target_logw):
     vmem = pl.BlockSpec(memory_space=pltpu.VMEM)
-    f_new, g_new, projection = pl.pallas_call(
+    out = pl.pallas_call(
         kernel,
-        out_shape=(
-            jax.ShapeDtypeStruct((1, OWN_ROWS), F32),
-            jax.ShapeDtypeStruct((1, OWN_COLS), F32),
-            jax.ShapeDtypeStruct((DIM, OWN_ROWS), F32),
-        ),
+        out_shape=jax.ShapeDtypeStruct((40, 128), F32),
         in_specs=[pl.BlockSpec(memory_space=pl.ANY)] * 5,
-        out_specs=(vmem,) * 3,
+        out_specs=vmem,
         scratch_shapes=[
             pltpu.VMEM((DIM, OWN_ROWS), F32),
             pltpu.VMEM((DIM, OWN_COLS), F32),
@@ -428,7 +388,7 @@
             pltpu.VMEM((24, 128), F32),
             pltpu.VMEM((40, 128), F32),
             pltpu.VMEM((GROUP, 24, 128), F32),
-            pltpu.VMEM((GROUP, 40, 128), F32),
+            pltpu.VMEM((2, 8, 40, 128), F32),
             pltpu.VMEM((256, ROWS), BF16),
             pltpu.VMEM((256, COLS), BF16),
             pltpu.VMEM((ROWS, 256), BF16),
@@ -466,6 +426,16 @@
         source_logw.reshape(1, OWN_ROWS),
         target_logw.reshape(1, OWN_COLS),
     )
+    f_new, g_new, projection = pl.pallas_call(
+        deliver,
+        out_shape=(
+            jax.ShapeDtypeStruct((1, OWN_ROWS), F32),
+            jax.ShapeDtypeStruct((1, OWN_COLS), F32),
+            jax.ShapeDtypeStruct((DIM, OWN_ROWS), F32),
+        ),
+        in_specs=[vmem],
+        out_specs=(vmem,) * 3,
+    )(out)
     return f_new.reshape(OWN_ROWS), g_new.reshape(OWN_COLS), projection
 
 

time: 43.2 us -> 40.8 us (0.944)
  local copies, waits for them, and re-layouts: 3.07 us -> 0 us
  Pallas kernels: 39.2 us -> 40 us
    unnamed x7 -> x0, local copies, waits for them, and re-layouts: 3.07 us -> none
    pallas_call x1 -> x2, Pallas kernels: 39.2 us -> 40 us  [the longest x1 38.6 us: body(): pl.pallas_call(kernel, out_shape=jax.ShapeDtypeStruct((40, 128), F32), in...]
where the time goes in v5:
time: 40.8 us; the launch traced here: 40.6 us
  Pallas kernels  40 us (98%)
  between operations  0.64 us (2%)
    pallas_call x1, Pallas kernels, body(): pl.pallas_call(kernel, out_shape=jax.ShapeDtypeStruct((40, 128), F32), in...  38.6 us
    pallas_call x1, Pallas kernels, body(): pl.pallas_call(deliver, out_shape=(jax.ShapeDtypeStruct((1, OWN_ROWS), F3...  1.34 us

profile of v5, /device:TPU:1, one launch (start us, length us, event | category | flops | bytes accessed | tf_op | source)
XLA Modules:
  0.0 40.6 jit_solution(1031191065866069942)
XLA Ops:
  0.6 38.6 %shard_map.76.out_ref = f32[40,128]{1,0:T(8,128)} custom-call(f32[32,64]{1,0:T(8,128)} %src_hbm.1, f32[32,104]{1,0:T(8,128)} %tgt_hbm.1, f32[1,104]{1,0:T(1,128)} %bitcast.5, f32[1,64]{1,0:T(1,128)} %bitcast.6, f32[1,104]{1,0:T(1,128)} %bitcast.7), custom_call_target="tpu_custom_call" | custom-call | tf_op jit(solution)/shard_map/pallas_call | solution.py:376
  39.3 1.3 %shard_map.77 = (f32[1,64]{1,0:T(1,128)}, f32[1,104]{1,0:T(1,128)}, f32[32,64]{1,0:T(8,128)}) custom-call(f32[40,128]{1,0:T(8,128)} %shard_map.76.out_ref), custom_call_target="tpu_custom_call" | custom-call | tf_op jit(solution)/shard_map/pallas_call | solution.py:429

commit v6 on v5

--- a/solution.py
+++ b/solution.py
@@ -91,7 +91,7 @@
     out_ref,
     src_v, tgt_v, pot_v, slw_v, tlw_v,
     pad, smsg, tmsg, srecv, trecv,
-    xr, yr, xt, yt, tl, ya, held, peak, scr,
+    xr, yr, xt, yt, tl, tf, wh, wl, ya, held, peak, scr,
     slw, tlw, lpart, lsend, lrecv, csend, crecv, gsend, grecv, msend, mrecv, lall, gall,
     in_sem, s_send, s_recv, t_send, t_recv, l_send, l_recv, g_send, g_recv, m_send, m_recv, c_send, c_recv,
 ):
@@ -251,9 +251,7 @@
         yr[192:208, at] = ones16
         yr[208:256, at] = zeros48
         yt[at, 0:128] = jnp.transpose(jnp.concatenate([y1, y2, y1, y2], 0)).astype(BF16)
-        tl[0:32, at] = y1.astype(BF16)
-        tl[32:48, at] = jnp.ones((16, 128), BF16)
-        tl[48:80, at] = y2.astype(BF16)
+        tf[:, at] = block[0:DIM]
 
     for offset in reversed(TGT_PEERS):
         slot = at_t(offset)
@@ -295,12 +293,26 @@
     )
     copy.start()
     sent.append(copy)
+    for q in range(13):
+        at = slice(128 * q, 128 * q + 128)
+        bias = tlw[q : q + 1, :] - csend[q : q + 1, :] - TOP_LOGW
+        tail = jnp.concatenate([yr[128:192, at].astype(F32), bias_rows(bias, 0, 1.0), zeros56], 0)
+        yt[at, 128:256] = jnp.transpose(tail).astype(BF16)
     arrive(there, c_recv.at[0])
     gsend[...] = combine([csend[...], crecv[...]])
     for n, z in enumerate(Z_PEERS):
         to_s((z, 0), me_z, gsend.at[0:13], grecv.at[me_z, 0:13], g_send.at[n], g_recv)
     grecv[me_z] = gsend[...]
 
+    orders = (2, 1, 3, 0)
+    for n, order in enumerate(orders):
+        columns = pl.ds(pl.multiple_of(lax.rem(me_y + order, 4) * 256, 256), 256)
+        for base, stop in ((0, 512), (512, 1024), (1024, 1664)):
+            weights = jnp.exp2(dot(yt[base:stop, :], xr[:, columns]))
+            high = weights.astype(BF16)
+            wh[n, base:stop, :] = high
+            wl[n, base:stop, :] = (weights - high.astype(F32)).astype(BF16)
+
     row = lall[pl.ds(me_y * 2 + me_x // 2, 1), :]
     row = jnp.where(lax.rem(me_t, 2) == 1, pltpu.roll(row, 64, 1), row)
     out_ref[32:33, :] = src_sq - (EPSILON / LOG2E) * row
@@ -310,37 +322,45 @@
         arrive(grecv.at[slot, 0:13], g_recv.at[slot])
     col_lse = combine([grecv[k] for k in range(8)])
     gall[...] = col_lse
+    factor = jnp.exp2(csend[...] - col_lse)
     for q in range(13):
         at = slice(128 * q, 128 * q + 128)
-        bias = tlw[q : q + 1, :] - col_lse[q : q + 1, :] - TOP_LOGW
-        tail = jnp.concatenate([yr[128:192, at].astype(F32), bias_rows(bias, 0, 1.0), zeros56], 0)
-        yt[at, 128:256] = jnp.transpose(tail).astype(BF16)
-    spans = ((0, 512), (512, 1024), (1024, 1664))
-    for order in (2, 1, 3, 0):
-        tile = lax.rem(me_y + order, 4)
-        columns = pl.ds(pl.multiple_of(tile * 256, 256), 256)
-        moments = None
-        for base, stop in spans:
-            weights = jnp.exp2(dot(yt[base:stop, :], xr[:, columns]))
-            high = weights.astype(BF16)
-            rest = (weights - high.astype(F32)).astype(BF16)
-            main = dot(tl[:, base:stop], high)
-            part = jnp.concatenate([main[0:32] + main[48:80], main[32:40]], 0)
-            part = part + dot(tl[0:48, base:stop], rest)[0:40]
-            moments = part if moments is None else moments + part
+        scale = factor[q : q + 1, :]
+        whole = tf[:, at] * scale
+        one = whole.astype(BF16)
+        scale_one = scale.astype(BF16).astype(F32)
+        sub = sub_iota(16)
+        line = jnp.where(sub == 0, scale_one, jnp.where(sub == 1, scale - scale_one, 0.0))
+        tl[0:32, at] = one
+        tl[32:48, at] = line.astype(BF16)
+        tl[48:80, at] = (whole - one.astype(F32)).astype(BF16)
+    def gather_moments(n):
+        tile = lax.rem(me_y + orders[n], 4)
+        main = dot(tl[...], wh[n])
+        rest = dot(tl[0:48, :], wl[n])
+        coords = main[0:32] + main[48:80] + rest[0:32]
+        norms = main[32:40] + rest[32:40]
+        norms = norms + pltpu.roll(norms, 7, 0)
         for u in range(4):
             lanes = slice(128 * (u // 2), 128 * (u // 2) + 128)
-            one, two, three = moments[0:16, lanes], moments[16:32, lanes], moments[32:40, lanes]
+            one, two, three = coords[0:16, lanes], coords[16:32, lanes], norms[:, lanes]
             if u % 2 == 0:
                 two = pltpu.roll(two, 64, 1)
             else:
                 one, three = pltpu.roll(one, 64, 1), pltpu.roll(three, 64, 1)
             msend[tile * 4 + u, 0:16, :] = jnp.where(low, one, two)
             msend[tile * 4 + u, 16:24, :] = three
-        for x in range(0 if order else 1, 4):
-            slot = tile * 4 + lax.rem(me_x + x, 4)
-            to_t((order, x), msend.at[slot, 0:SRC_LINES], mrecv.at[me_t, 0:SRC_LINES],
-                 m_send.at[order * 4 + x], m_recv)
+
+    for group in ((0, 1), (2, 3)):
+        for n in group:
+            gather_moments(n)
+        for n in group:
+            order = orders[n]
+            tile = lax.rem(me_y + order, 4)
+            for x in range(0 if order else 1, 4):
+                slot = tile * 4 + lax.rem(me_x + x, 4)
+                to_t((order, x), msend.at[slot, 0:SRC_LINES], mrecv.at[me_t, 0:SRC_LINES],
+                     m_send.at[order * 4 + x], m_recv)
     mrecv[me_t] = msend[me_t]
 
     start = me_s * OWN_COLS
@@ -394,10 +414,13 @@
             pltpu.VMEM((ROWS, 256), BF16),
             pltpu.VMEM((COLS, 256), BF16),
             pltpu.VMEM((80, COLS), BF16),
+            pltpu.VMEM((DIM, COLS), F32),
+            pltpu.VMEM((4, COLS, 256), BF16),
+            pltpu.VMEM((4, COLS, 256), BF16),
             pltpu.VMEM((8, 2 * OWN_COLS, 256), BF16),
             pltpu.VMEM((2, 2 * OWN_COLS, ROWS), F32),
             pltpu.VMEM((2, 1, ROWS), F32),
-            pltpu.VMEM((2, COLS, 256), F32),
+            pltpu.VMEM((2, ROWS, 256), F32),
             pltpu.VMEM((8, 128), F32),
             pltpu.VMEM((16, 128), F32),
             pltpu.VMEM((8, 8, 128), F32),

time: 40.8 us -> 39.1 us (0.958)
  Pallas kernels: 40 us -> 38.3 us
    pallas_call x1, Pallas kernels: 38.6 us -> 37 us  [body(): pl.pallas_call(kernel, out_shape=jax.ShapeDtypeStruct((40, 128), F32), in...]
where the time goes in v6:
time: 39.1 us; the launch traced here: 39 us
  Pallas kernels  38.3 us (98%)
  between operations  0.64 us (2%)
    pallas_call x1, Pallas kernels, body(): pl.pallas_call(kernel, out_shape=jax.ShapeDtypeStruct((40, 128), F32), in...  37 us
    pallas_call x1, Pallas kernels, body(): pl.pallas_call(deliver, out_shape=(jax.ShapeDtypeStruct((1, OWN_ROWS), F3...  1.34 us

profile of v6, /device:TPU:1, one launch (start us, length us, event | category | flops | bytes accessed | tf_op | source)
XLA Modules:
  0.0 39.0 jit_solution(9800463412850950221)
XLA Ops:
  0.6 37.0 %shard_map.76.out_ref = f32[40,128]{1,0:T(8,128)} custom-call(f32[32,64]{1,0:T(8,128)} %src_hbm.1, f32[32,104]{1,0:T(8,128)} %tgt_hbm.1, f32[1,104]{1,0:T(1,128)} %bitcast.5, f32[1,64]{1,0:T(1,128)} %bitcast.6, f32[1,104]{1,0:T(1,128)} %bitcast.7), custom_call_target="tpu_custom_call" | custom-call | tf_op jit(solution)/shard_map/pallas_call | solution.py:396
  37.6 1.3 %shard_map.77 = (f32[1,64]{1,0:T(1,128)}, f32[1,104]{1,0:T(1,128)}, f32[32,64]{1,0:T(8,128)}) custom-call(f32[40,128]{1,0:T(8,128)} %shard_map.76.out_ref), custom_call_target="tpu_custom_call" | custom-call | tf_op jit(solution)/shard_map/pallas_call | solution.py:452

commit v7 on v6

--- a/solution.py
+++ b/solution.py
@@ -92,7 +92,7 @@
     src_v, tgt_v, pot_v, slw_v, tlw_v,
     pad, smsg, tmsg, srecv, trecv,
     xr, yr, xt, yt, tl, tf, wh, wl, ya, held, peak, scr,
-    slw, tlw, lpart, lsend, lrecv, csend, crecv, gsend, grecv, msend, mrecv, lall, gall,
+    slw, tlw, lpart, lsend, lrecv, cpart, csend, crecv, gsend, grecv, msend, mrecv, lall, gall,
     in_sem, s_send, s_recv, t_send, t_recv, l_send, l_recv, g_send, g_recv, m_send, m_recv, c_send, c_recv,
 ):
     me_t = lax.axis_index("tgt")
@@ -107,10 +107,10 @@
         return lax.rem(me_z + offset[0], 8) * 2 + lax.rem(me_c + offset[1], 2)
 
     barrier = pltpu.get_barrier_semaphore()
+    for offset in [(z, 0) for z in Z_PEERS] + [(0, 1)]:
+        pl.semaphore_signal(barrier, inc=1, device_id={"src": at_s(offset)}, device_id_type=MESH)
     for offset in TGT_PEERS:
         pl.semaphore_signal(barrier, inc=1, device_id={"tgt": at_t(offset)}, device_id_type=MESH)
-    for offset in [(z, 0) for z in Z_PEERS] + [(0, 1)]:
-        pl.semaphore_signal(barrier, inc=1, device_id={"src": at_s(offset)}, device_id_type=MESH)
 
     inputs = [
         pltpu.make_async_copy(a, b, in_sem.at[n])
@@ -185,16 +185,11 @@
         ya[n, :, 0:128] = jnp.concatenate(tops_t, 0).astype(BF16)
         ya[n, :, 128:256] = jnp.concatenate(tails_t, 0).astype(BF16)
 
-    def first(n):
-        scores = dot(ya[n], xr[...])
-        held[n % 2] = scores
-        peak[n % 2] = jnp.max(scores, 0, keepdims=True)
-
     def second(n):
-        top = peak[n % 2]
-        part = top + jnp.log(jnp.sum(jnp.exp2(held[n % 2] - top), 0, keepdims=True)) * LOG2E
-        for p in range(8):
-            lpart[n, p : p + 1, :] = part[:, 128 * p : 128 * p + 128]
+        for t in range(4):
+            part = lse(dot(ya[n], xr[:, 256 * t : 256 * t + 256]))
+            lpart[n, 2 * t : 2 * t + 1, :] = part[:, 0:128]
+            lpart[n, 2 * t + 1 : 2 * t + 2, :] = part[:, 128:256]
 
     for z in reversed(Z_PEERS):
         arrive(trecv.at[0, 8 - z, 0:TGT_LINES], t_recv.at[8 - z])
@@ -215,17 +210,14 @@
         xr[128:192, at] = jnp.concatenate([x1, x3], 0).astype(BF16)
         xr[192:208, at] = ones16
         xr[208:256, at] = zeros48
-    first(0)
+    second(0)
     for n in range(1, 4):
         operand(n)
-        first(n)
-        second(n - 1)
+        second(n)
     arrive(trecv.at[1, :, 0:TGT_LINES], t_recv.at[8])
     for n in range(4, 8):
         operand(n)
-        first(n)
-        second(n - 1)
-    second(7)
+        second(n)
     lsend[...] = combine([lpart[n] for n in range(8)])
     for n, offset in enumerate(TGT_PEERS):
         to_t(offset, lsend, lrecv.at[me_t], l_send.at[n], l_recv)
@@ -266,26 +258,18 @@
         both = jnp.concatenate([bias_rows(bias, 3, 1.0), jnp.zeros((8, 128), F32)], 0)
         xr[192:208, at] = both.astype(BF16)
 
-    def first(n):
-        width = min(256, COLS - 256 * n)
-        scores = dot(xt[...], yr[:, 256 * n : 256 * n + width])
-        scr[n % 2, 0:ROWS, 0:width] = scores
-        peak[n % 2, :, 0:width] = jnp.max(scores, 0, keepdims=True)
-
-    def second(n):
-        width = min(256, COLS - 256 * n)
-        top = peak[n % 2, :, 0:width]
-        part = top + jnp.log(
-            jnp.sum(jnp.exp2(scr[n % 2, 0:ROWS, 0:width] - top), 0, keepdims=True)
-        ) * LOG2E
-        for h in range(width // 128):
-            csend[2 * n + h : 2 * n + h + 1, :] = part[:, 128 * h : 128 * h + 128]
-
-    for n in range(8):
-        if n < 7:
-            first(n)
-        if n > 0:
-            second(n - 1)
+    def block_rows(r, carry):
+        rows = xt[pl.ds(pl.multiple_of(r * 256, 256), 256), :]
+        for n in range(7):
+            width = min(256, COLS - 256 * n)
+            part = lse(dot(rows, yr[:, 256 * n : 256 * n + width]))
+            for h in range(width // 128):
+                cpart[r, 2 * n + h : 2 * n + h + 1, :] = part[:, 128 * h : 128 * h + 128]
+        return carry
+
+    for r in range(4):
+        block_rows(r, 0)
+    csend[...] = combine([cpart[r] for r in range(4)])
     there = crecv.at[0:13]
     copy = pltpu.make_async_remote_copy(
         src_ref=csend.at[0:13], dst_ref=there, send_sem=c_send.at[0], recv_sem=c_recv.at[0],
@@ -395,7 +379,7 @@
     vmem = pl.BlockSpec(memory_space=pltpu.VMEM)
     out = pl.pallas_call(
         kernel,
-        out_shape=jax.ShapeDtypeStruct((40, 128), F32),
+        out_shape=pltpu.VMEM((40, 128), F32),
         in_specs=[pl.BlockSpec(memory_space=pl.ANY)] * 5,
         out_specs=vmem,
         scratch_shapes=[
@@ -426,6 +410,7 @@
             pltpu.VMEM((8, 8, 128), F32),
             pltpu.VMEM((8, 128), F32),
             pltpu.VMEM((GROUP, 8, 128), F32),
+            pltpu.VMEM((4, 16, 128), F32),
             pltpu.VMEM((16, 128), F32),
             pltpu.VMEM((16, 128), F32),
             pltpu.VMEM((16, 128), F32),
@@ -458,7 +443,7 @@
         ),
         in_specs=[vmem],
         out_specs=(vmem,) * 3,
-    )(out)
+    )(pltpu.with_memory_space_constraint(out, pltpu.VMEM))
     return f_new.reshape(OWN_ROWS), g_new.reshape(OWN_COLS), projection
 
 

time: 39.1 us -> 37.4 us (0.957)
  Pallas kernels: 38.3 us -> 36.6 us
    pallas_call x1, Pallas kernels: 37 us -> 36 us  [body(): pl.pallas_call(kernel, out_shape=pltpu.VMEM((40, 128), F32), in_specs=[pl...]
    pallas_call x1, Pallas kernels: 1.34 us -> 0.62 us  [body(): pl.pallas_call(deliver, out_shape=(jax.ShapeDtypeStruct((1, OWN_ROWS), F3...]
where the time goes in v7:
time: 37.4 us; the launch traced here: 37.2 us
  Pallas kernels  36.6 us (98%)
  between operations  0.64 us (2%)
    pallas_call x1, Pallas kernels, body(): pl.pallas_call(kernel, out_shape=pltpu.VMEM((40, 128), F32), in_specs=[pl...  36 us

profile of v7, /device:TPU:1, one launch (start us, length us, event | category | flops | bytes accessed | tf_op | source)
XLA Modules:
  0.0 37.2 jit_solution(9404547596763547607)
XLA Ops:
  0.6 36.0 %shard_map.76.out_ref = f32[40,128]{1,0:T(8,128)S(1)} custom-call(f32[32,64]{1,0:T(8,128)} %src_hbm.1, f32[32,104]{1,0:T(8,128)} %tgt_hbm.1, f32[1,104]{1,0:T(1,128)} %bitcast.5, f32[1,64]{1,0:T(1,128)} %bitcast.6, f32[1,104]{1,0:T(1,128)} %bitcast.7), custom_call_target="tpu_custom_call" | custom-call | tf_op jit(solution)/shard_map/pallas_call | solution.py:380
  36.6 0.6 %shard_map.77 = (f32[1,64]{1,0:T(1,128)}, f32[1,104]{1,0:T(1,128)}, f32[32,64]{1,0:T(8,128)}) custom-call(f32[40,128]{1,0:T(8,128)S(1)} %shard_map.76.out_ref), custom_call_target="tpu_custom_call" | custom-call | tf_op jit(solution)/shard_map/pallas_call | solution.py:437

commit v8 on v7

--- a/solution.py
+++ b/solution.py
@@ -335,7 +335,7 @@
             msend[tile * 4 + u, 0:16, :] = jnp.where(low, one, two)
             msend[tile * 4 + u, 16:24, :] = three
 
-    for group in ((0, 1), (2, 3)):
+    for group in ((0, 1, 2), (3,)):
         for n in group:
             gather_moments(n)
         for n in group:

time: 37.4 us -> 37.8 us (1.011)
  Pallas kernels: 36.6 us -> 37 us
    pallas_call x1, Pallas kernels: 36 us -> 36.3 us  [body(): pl.pallas_call(kernel, out_shape=pltpu.VMEM((40, 128), F32), in_specs=[pl...]
where the time goes in v8:
time: 37.8 us; the launch traced here: 37.6 us
  Pallas kernels  37 us (98%)
  between operations  0.64 us (2%)
    pallas_call x1, Pallas kernels, body(): pl.pallas_call(kernel, out_shape=pltpu.VMEM((40, 128), F32), in_specs=[pl...  36.3 us

profile of v8, /device:TPU:1, one launch (start us, length us, event | category | flops | bytes accessed | tf_op | source)
XLA Modules:
  0.0 37.6 jit_solution(13662719643029473380)
XLA Ops:
  0.6 36.3 %shard_map.76.out_ref = f32[40,128]{1,0:T(8,128)S(1)} custom-call(f32[32,64]{1,0:T(8,128)} %src_hbm.1, f32[32,104]{1,0:T(8,128)} %tgt_hbm.1, f32[1,104]{1,0:T(1,128)} %bitcast.5, f32[1,64]{1,0:T(1,128)} %bitcast.6, f32[1,104]{1,0:T(1,128)} %bitcast.7), custom_call_target="tpu_custom_call" | custom-call | tf_op jit(solution)/shard_map/pallas_call | solution.py:380
  37.0 0.6 %shard_map.77 = (f32[1,64]{1,0:T(1,128)}, f32[1,104]{1,0:T(1,128)}, f32[32,64]{1,0:T(8,128)}) custom-call(f32[40,128]{1,0:T(8,128)S(1)} %shard_map.76.out_ref), custom_call_target="tpu_custom_call" | custom-call | tf_op jit(solution)/shard_map/pallas_call | solution.py:437

commit v9 on v7

--- a/solution.py
+++ b/solution.py
@@ -91,7 +91,7 @@
     out_ref,
     src_v, tgt_v, pot_v, slw_v, tlw_v,
     pad, smsg, tmsg, srecv, trecv,
-    xr, yr, xt, yt, tl, tf, wh, wl, ya, held, peak, scr,
+    xr, yr, xt, yt, tl, tf, cross, wh, wl, ya, held, peak, scr,
     slw, tlw, lpart, lsend, lrecv, cpart, csend, crecv, gsend, grecv, msend, mrecv, lall, gall,
     in_sem, s_send, s_recv, t_send, t_recv, l_send, l_recv, g_send, g_recv, m_send, m_recv, c_send, c_recv,
 ):
@@ -245,31 +245,35 @@
         yt[at, 0:128] = jnp.transpose(jnp.concatenate([y1, y2, y1, y2], 0)).astype(BF16)
         tf[:, at] = block[0:DIM]
 
+    for p in range(8):
+        at = slice(128 * p, 128 * p + 128)
+        tail = jnp.concatenate([xr[128:192, at].astype(F32), jnp.zeros((64, 128), F32)], 0)
+        xt[at, 128:256] = jnp.transpose(tail).astype(BF16)
+    for r in range(4):
+        rows = slice(256 * r, 256 * r + 256)
+        for n in range(7):
+            columns = slice(256 * n, min(256 * n + 256, COLS))
+            cross[rows, columns] = dot(xt[rows, :], yr[:, columns])
+
     for offset in reversed(TGT_PEERS):
         slot = at_t(offset)
         arrive(lrecv.at[slot], l_recv.at[slot])
     row_lse = combine([lrecv[k] for k in range(GROUP)])
     lall[...] = row_lse
-    for p in range(8):
-        at = slice(128 * p, 128 * p + 128)
-        bias = slw[p : p + 1, :] - row_lse[p : p + 1, :]
-        tail = jnp.concatenate([xr[128:192, at].astype(F32), bias_rows(bias), zeros56], 0)
-        xt[at, 128:256] = jnp.transpose(tail).astype(BF16)
-        both = jnp.concatenate([bias_rows(bias, 3, 1.0), jnp.zeros((8, 128), F32)], 0)
-        xr[192:208, at] = both.astype(BF16)
-
-    def block_rows(r, carry):
-        rows = xt[pl.ds(pl.multiple_of(r * 256, 256), 256), :]
+    bias = slw[...] - row_lse
+
+    for r in range(8):
+        tall = jnp.transpose(jnp.broadcast_to(bias[r : r + 1, :], (128, 128)))
         for n in range(7):
             width = min(256, COLS - 256 * n)
-            part = lse(dot(rows, yr[:, 256 * n : 256 * n + width]))
-            for h in range(width // 128):
-                cpart[r, 2 * n + h : 2 * n + h + 1, :] = part[:, 128 * h : 128 * h + 128]
-        return carry
-
-    for r in range(4):
-        block_rows(r, 0)
-    csend[...] = combine([cpart[r] for r in range(4)])
+            columns = slice(256 * n, 256 * n + width)
+            here = cross[128 * r : 128 * r + 128, columns] + jnp.concatenate([tall] * (width // 128), 1)
+            here = here.reshape(16, 8, width)
+            top = jnp.max(here, 0)
+            cpart[r, :, columns] = top + jnp.log(jnp.sum(jnp.exp2(here - top), 0)) * LOG2E
+    for q in range(13):
+        columns = slice(128 * q, 128 * q + 128)
+        csend[q : q + 1, :] = lse(cpart[:, :, columns].reshape(64, 128))
     there = crecv.at[0:13]
     copy = pltpu.make_async_remote_copy(
         src_ref=csend.at[0:13], dst_ref=there, send_sem=c_send.at[0], recv_sem=c_recv.at[0],
@@ -277,6 +281,10 @@
     )
     copy.start()
     sent.append(copy)
+    for p in range(8):
+        at = slice(128 * p, 128 * p + 128)
+        both = jnp.concatenate([bias_rows(bias[p : p + 1, :], 3, 1.0), jnp.zeros((8, 128), F32)], 0)
+        xr[192:208, at] = both.astype(BF16)
     for q in range(13):
         at = slice(128 * q, 128 * q + 128)
         bias = tlw[q : q + 1, :] - csend[q : q + 1, :] - TOP_LOGW
@@ -399,6 +407,7 @@
             pltpu.VMEM((COLS, 256), BF16),
             pltpu.VMEM((80, COLS), BF16),
             pltpu.VMEM((DIM, COLS), F32),
+            pltpu.VMEM((ROWS, COLS), F32),
             pltpu.VMEM((4, COLS, 256), BF16),
             pltpu.VMEM((4, COLS, 256), BF16),
             pltpu.VMEM((8, 2 * OWN_COLS, 256), BF16),
@@ -410,7 +419,7 @@
             pltpu.VMEM((8, 8, 128), F32),
             pltpu.VMEM((8, 128), F32),
             pltpu.VMEM((GROUP, 8, 128), F32),
-            pltpu.VMEM((4, 16, 128), F32),
+            pltpu.VMEM((8, 8, COLS), F32),
             pltpu.VMEM((16, 128), F32),
             pltpu.VMEM((16, 128), F32),
             pltpu.VMEM((16, 128), F32),

time: 37.4 us -> 37.2 us (level)
  no operation moved by 1% of the time
where the time goes in v9:
time: 37.2 us; the launch traced here: 37.1 us
  Pallas kernels  36.4 us (98%)
  between operations  0.64 us (2%)
    pallas_call x1, Pallas kernels, body(): pl.pallas_call(kernel, out_shape=pltpu.VMEM((40, 128), F32), in_specs=[pl...  35.8 us

profile of v9, /device:TPU:1, one launch (start us, length us, event | category | flops | bytes accessed | tf_op | source)
XLA Modules:
  0.0 37.1 jit_solution(3281340237612261548)
XLA Ops:
  0.6 35.8 %shard_map.76.out_ref = f32[40,128]{1,0:T(8,128)S(1)} custom-call(f32[32,64]{1,0:T(8,128)} %src_hbm.1, f32[32,104]{1,0:T(8,128)} %tgt_hbm.1, f32[1,104]{1,0:T(1,128)} %bitcast.5, f32[1,64]{1,0:T(1,128)} %bitcast.6, f32[1,104]{1,0:T(1,128)} %bitcast.7), custom_call_target="tpu_custom_call" | custom-call | tf_op jit(solution)/shard_map/pallas_call | solution.py:388
  36.5 0.6 %shard_map.77 = (f32[1,64]{1,0:T(1,128)}, f32[1,104]{1,0:T(1,128)}, f32[32,64]{1,0:T(8,128)}) custom-call(f32[40,128]{1,0:T(8,128)S(1)} %shard_map.76.out_ref), custom_call_target="tpu_custom_call" | custom-call | tf_op jit(solution)/shard_map/pallas_call | solution.py:446
